TPU v7x, 512 devices: a whole 4x8x8 slice. The times are simulated.
512 devices in a mesh: dp: 16 (over y_lo, z), gx: 8 (over x, core), gy: 4 (over y_hi).
Axes of the slice: x: 4, y: 8 (y_hi: 4, y_lo: 2; y = y_hi * 2 + y_lo), z: 8, core: 2. Of those that a mesh axis runs over, the one named last changes fastest.
Arguments:
- fields: bfloat16 [16, 20, 32, 16384], P('dp', None, None, ('gx', 'gy')), may hold values from -6 to 6
- cotangent: bfloat16 [16, 20, 32, 16384], P('dp', None, None, ('gx', 'gy')), may hold values from -6 to 6
- mix_weight: bfloat16 [20, 20], replicated, may hold values from -1.25 to 1.25
- spectral_weight: bfloat16 [288, 2, 20, 20], P(('gx', 'gy')), may hold values from -1 to 1
Outputs:
- output: bfloat16 [16, 20, 32, 16384], P('dp', None, None, ('gx', 'gy'))
- spectral_grad: float32 [288, 2, 20, 20], P(('gx', 'gy'))
- mixing_grad: float32 [20, 20], replicated
All inputs are finite; a program needn't handle non-finite values.
Results may differ from a plain program's by a relative error of at most 0.0031.
Values may be sent and summed in bfloat16 or wider, within the bound.
A program may use at most 64 MiB of HBM per device.

v0:
```python
import math

import jax
import jax.numpy as jnp
from jax import lax
from jax.sharding import PartitionSpec as P

NX = 128
NY = 128
KX = 24
KY = 12
P_SIZE = 32
MODES = 288


HI = lax.Precision.HIGHEST


def gelu_value(h):
    k = math.sqrt(2.0 / math.pi)
    t = jnp.tanh(k * (h + 0.044715 * h * h * h))
    return 0.5 * h * (1.0 + t)


def gelu_slope(h):
    k = math.sqrt(2.0 / math.pi)
    t = jnp.tanh(k * (h + 0.044715 * h * h * h))
    return 0.5 * (1.0 + t) + 0.5 * h * (1.0 - t * t) * k * (1.0 + 3.0 * 0.044715 * h * h)


def axis_table(waves, n):
    cells = jnp.arange(n, dtype=jnp.int32)
    angle = 2.0 * math.pi / n * (waves[:, None] * cells[None, :] % n).astype(jnp.float32)
    return (jnp.cos(angle), jnp.sin(angle))


def tables():
    index = jnp.arange(KX, dtype=jnp.int32)
    waves_x = jnp.where(index < KX // 2, index, NX - KX + index)
    cos_x, sin_x = axis_table(waves_x, NX)
    cos_y, sin_y = axis_table(jnp.arange(KY, dtype=jnp.int32), NY)
    return (cos_x, sin_x, cos_y, sin_y)


def forward_dft(data, scale):
    cos_x, sin_x, cos_y, sin_y = tables()
    a_re = jnp.einsum("cpxy,ky->cpxk", data, cos_y, precision=HI)
    a_im = -jnp.einsum("cpxy,ky->cpxk", data, sin_y, precision=HI)
    s_re = jnp.einsum("cpxk,jx->jkcp", a_re, cos_x, precision=HI) + jnp.einsum(
        "cpxk,jx->jkcp", a_im, sin_x, precision=HI
    )
    s_im = jnp.einsum("cpxk,jx->jkcp", a_im, cos_x, precision=HI) - jnp.einsum(
        "cpxk,jx->jkcp", a_re, sin_x, precision=HI
    )
    chans, planes = (data.shape[0], data.shape[1])
    return scale * jnp.stack(
        [s_re.reshape(MODES, chans, planes), s_im.reshape(MODES, chans, planes)], axis=1
    )


def inverse_dft(vals, scale):
    cos_x, sin_x, cos_y, sin_y = tables()
    chans, planes = (vals.shape[2], vals.shape[3])
    v_re = vals[:, 0].reshape(KX, KY, chans, planes)
    v_im = vals[:, 1].reshape(KX, KY, chans, planes)
    b_re = jnp.einsum("jkdp,jx->dpxk", v_re, cos_x, precision=HI) - jnp.einsum(
        "jkdp,jx->dpxk", v_im, sin_x, precision=HI
    )
    b_im = jnp.einsum("jkdp,jx->dpxk", v_re, sin_x, precision=HI) + jnp.einsum(
        "jkdp,jx->dpxk", v_im, cos_x, precision=HI
    )
    return scale * (
        jnp.einsum("dpxk,ky->dpxy", b_re, cos_y, precision=HI)
        - jnp.einsum("dpxk,ky->dpxy", b_im, sin_y, precision=HI)
    )


def spectral_mix(spec, weight):
    w = weight.astype(jnp.float32)
    v_re = jnp.einsum("mcp,mcd->mdp", spec[:, 0], w[:, 0], precision=HI) - jnp.einsum(
        "mcp,mcd->mdp", spec[:, 1], w[:, 1], precision=HI
    )
    v_im = jnp.einsum("mcp,mcd->mdp", spec[:, 0], w[:, 1], precision=HI) + jnp.einsum(
        "mcp,mcd->mdp", spec[:, 1], w[:, 0], precision=HI
    )
    return jnp.stack([v_re, v_im], axis=1)


def grads_of(spec, gspec):
    g_re = jnp.einsum("mcp,mdp->mcd", spec[:, 0], gspec[:, 0], precision=HI) + jnp.einsum(
        "mcp,mdp->mcd", spec[:, 1], gspec[:, 1], precision=HI
    )
    g_im = jnp.einsum("mcp,mdp->mcd", spec[:, 0], gspec[:, 1], precision=HI) - jnp.einsum(
        "mcp,mdp->mcd", spec[:, 1], gspec[:, 0], precision=HI
    )
    return jnp.stack([g_re, g_im], axis=1)


def to_planes(block):
    chans, planes, rows_x, full_y = block.shape
    size_x = lax.axis_size("gx")
    size_y = lax.axis_size("gy")
    moved = lax.all_to_all(
        lax.all_to_all(block, "gx", split_axis=1, concat_axis=2, tiled=True),
        "gy",
        split_axis=1,
        concat_axis=2,
        tiled=True,
    )
    own = moved.shape[1]
    moved = moved.reshape(chans, own, size_y, size_x, rows_x, full_y)
    moved = jnp.transpose(moved, (0, 1, 3, 2, 4, 5))
    return moved.reshape(chans, own, size_x * size_y * rows_x, full_y)


def to_cells(plane_block):
    chans, own, full_x, full_y = plane_block.shape
    size_x = lax.axis_size("gx")
    size_y = lax.axis_size("gy")
    rows_x = full_x // (size_x * size_y)
    moved = lax.all_to_all(
        lax.all_to_all(plane_block, "gx", split_axis=2, concat_axis=1, tiled=True),
        "gy",
        split_axis=2,
        concat_axis=1,
        tiled=True,
    )
    moved = moved.reshape(chans, size_y, size_x, own, rows_x, full_y)
    moved = jnp.transpose(moved, (0, 2, 1, 3, 4, 5))
    return moved.reshape(chans, size_x * size_y * own, rows_x, full_y)


def local(fields, cotangent, mix_weight, spectral_weight):
    flat = fields[0]
    grad_out = cotangent[0].astype(jnp.float32)
    chans, planes, cells = flat.shape
    rows_x = cells // NY
    norm_in = 1.0 / math.sqrt(NX * NY)
    norm_out = 1.0 / math.sqrt(MODES)
    samples = lax.axis_size("dp")
    mixed = jnp.einsum("cpq,cd->dpq", flat, mix_weight, preferred_element_type=jnp.float32)
    plane_field = to_planes(flat.reshape(chans, planes, rows_x, NY)).astype(jnp.float32)
    spec = forward_dft(plane_field, norm_in)
    full_weight = lax.all_gather(spectral_weight, ("gx", "gy"), axis=0, tiled=True)
    vals = spectral_mix(spec, full_weight)
    branch = to_cells(inverse_dft(vals, norm_out)).reshape(chans, planes, cells)
    pre = branch + mixed
    output = gelu_value(pre).astype(jnp.bfloat16).reshape(1, chans, planes, cells)
    back = (grad_out * gelu_slope(pre)).astype(jnp.bfloat16)
    local_mix = jnp.einsum("cpq,dpq->cd", flat, back, preferred_element_type=jnp.float32)
    mix_scale = 1.0 / math.sqrt(samples * P_SIZE * NX * NY)
    spec_scale = 1.0 / math.sqrt(samples * P_SIZE)
    plane_back = to_planes(back.reshape(chans, planes, rows_x, NY)).astype(jnp.float32)
    gspec = forward_dft(plane_back, norm_out)
    local_spec = grads_of(spec, gspec)
    share = lax.psum_scatter(local_spec, ("gx", "gy"), scatter_dimension=0, tiled=True)
    spectral_grad = lax.psum(share, "dp") * spec_scale
    mixing_grad = lax.psum(local_mix, ("dp", "gx", "gy")) * mix_scale
    return (output, spectral_grad, mixing_grad)


def solution(mesh):
    return jax.shard_map(
        local,
        mesh=mesh,
        in_specs=(
            P("dp", None, None, ("gx", "gy")),
            P("dp", None, None, ("gx", "gy")),
            P(),
            P(("gx", "gy"), None, None, None),
        ),
        out_specs=(P("dp", None, None, ("gx", "gy")), P(("gx", "gy"), None, None, None), P()),
        check_vma=False,
    )
```

profile of v0, /device:TPU:1, one launch (start us, length us, event | category | flops | bytes accessed | tf_op | source)
XLA Modules:
  0.0 700.2 jit_solution(4944024013968660867)
XLA Ops:
  7.2 1.6 reshape_squeeze.3
  8.8 1.1 copy.251
  9.9 10.9 %all-to-all-start = ((bf16[20,32,4,128]{3,2,0,1:T(4,128)(2,1)}), bf16[20,32,4,128]{3,2,0,1:T(4,128)(2,1)}, u32[]{:S(2)}, u32[]{:S(2)}) async-start(bf16[20,32,4,128]{3,2,0,1:T(4,128)(2,1)} %copy.251), calls=%async_computation | async-start | bytes 1310720 | tf_op jit(solution)/shard_map/all_to_all | solution.py:104
  20.8 112.8 %all_gather.3 = bf16[288,2,20,20]{3,1,2,0:T(2,128)(2,1)S(1)} all-gather(bf16[9,2,20,20]{3,1,2,0:T(2,128)(2,1)S(1)} %copy-done.5), channel_id=1, replica_groups=mesh['dp'=16,'gx'=8,'gy'=4] {'gx','gy'}, dimensions={0}, use_global_device_ids=true | all-gather | bytes 475200 | tf_op jit(solution)/shard_map/all_gather | solution.py:144
  133.6 1.3 copy.252
  136.2 4.4 all-to-all-start.1
  140.5 5.6 fusion.165
  146.2 6.4 copy.317
  152.6 4.7 copy.318
  157.2 1.2 copy.255
  167.4 2.2 fusion.24
  169.7 2.2 fusion.8
  171.9 1.3 copy.271
  173.3 23.5 %all_to_all.81 = f32[20,1,128,128]{3,1,0,2:T(1,128)S(1)} all-to-all(f32[20,1,128,128]{3,1,0,2:T(1,128)S(1)} %copy.271), channel_id=1, replica_groups=mesh['dp'=16,'gx'=8,'gy'=4] {'gx'}, dimensions={2} | all-to-all | bytes 2621440 | tf_op jit(solution)/shard_map/all_to_all | solution.py:122
  197.4 38.2 %all_to_all.82 = f32[20,8,16,128]{3,1,0,2:T(8,128)S(1)} all-to-all(f32[20,8,16,128]{3,1,0,2:T(8,128)S(1)} %copy.273), channel_id=1, replica_groups=mesh['dp'=16,'gx'=8,'gy'=4] {'gy'}, dimensions={2} | all-to-all | bytes 2621440 | tf_op jit(solution)/shard_map/all_to_all | solution.py:121
  237.5 4.7 fusion.6
  242.5 15.5 %all_to_all.83 = bf16[20,32,4,128]{3,2,0,1:T(4,128)(2,1)S(1)} all-to-all(bf16[20,32,4,128]{3,2,0,1:T(4,128)(2,1)S(1)} %reshape.261), channel_id=1, replica_groups=mesh['dp'=16,'gx'=8,'gy'=4] {'gx'}, dimensions={1} | all-to-all | bytes 1310720 | tf_op jit(solution)/shard_map/all_to_all | solution.py:104
  258.3 20.1 %all_to_all.84 = bf16[20,4,32,128]{3,2,0,1:T(8,128)(2,1)S(1)} all-to-all(bf16[20,4,32,128]{3,2,0,1:T(8,128)(2,1)S(1)} %copy.282), channel_id=1, replica_groups=mesh['dp'=16,'gx'=8,'gy'=4] {'gy'}, dimensions={1} | all-to-all | bytes 1310720 | tf_op jit(solution)/shard_map/all_to_all | solution.py:103
  285.2 6.0 copy.290
  291.2 1.3 dynamic-slice
  293.2 1.0 copy.292
  295.0 107.2 %psum.15 = f32[20,20]{0,1:T(8,128)S(1)} all-reduce(f32[20,20]{0,1:T(8,128)S(1)} %convolution_bitcast_fusion.1), channel_id=1, replica_groups=mesh['dp'=16,'gx'=8,'gy'=4] {'dp','gx','gy'}, use_global_device_ids=true, to_apply=%region_2.3 | all-reduce | flops 400 | bytes 3200 | tf_op jit(solution)/shard_map/psum | solution.py:158
  402.8 234.0 %all-reduce.3.cloned.1.call-done = f32[288,2,20,20]{3,1,2,0:T(2,128)} async-done(((f32[288,2,20,20]{3,1,2,0:T(2,128)}), f32[288,2,20,20]{3,1,2,0:T(2,128)}) %all-reduce.3.cloned.1.call-update) | async-done | bytes 921616
  637.8 54.8 %psum.14 = f32[9,2,20,20]{3,1,2,0:T(2,128)S(1)} all-reduce(f32[9,2,20,20]{3,1,2,0:T(2,128)S(1)} %constant_dynamic-slice_fusion), channel_id=1, replica_groups=mesh['dp'=16,'gx'=8,'gy'=4] {'dp'}, use_global_device_ids=true, to_apply=%region_1.2 | all-reduce | flops 7200 | bytes 57600 | tf_op jit(solution)/shard_map/psum | solution.py:157
  (74 shorter events, 23.1 us)
Async XLA Ops:
  7.2 229.8 %copy-start = (bf16[20,20]{1,0:T(8,128)(2,1)S(1)}, bf16[20,20]{1,0:T(8,128)(2,1)}, u32[]{:S(2)}) copy-start(bf16[20,20]{1,0:T(8,128)(2,1)} %param.6) | copy-start | bytes 2404
  8.8 12.0 %copy-start.5 = (bf16[9,2,20,20]{3,1,2,0:T(2,128)(2,1)S(1)}, bf16[9,2,20,20]{3,1,2,0:T(2,128)(2,1)}, u32[]{:S(2)}) copy-start(bf16[9,2,20,20]{3,1,2,0:T(2,128)(2,1)} %param.7) | copy-start | bytes 43204
  9.9 123.7 %all-to-all-start = ((bf16[20,32,4,128]{3,2,0,1:T(4,128)(2,1)}), bf16[20,32,4,128]{3,2,0,1:T(4,128)(2,1)}, u32[]{:S(2)}, u32[]{:S(2)}) async-start(bf16[20,32,4,128]{3,2,0,1:T(4,128)(2,1)} %copy.251), calls=%async_computation | async-start | bytes 1310720 | tf_op jit(solution)/shard_map/all_to_all | solution.py:104
  136.2 21.1 %all-to-all-start.1 = ((bf16[20,4,32,128]{3,2,0,1:T(8,128)(2,1)}), bf16[20,4,32,128]{3,2,0,1:T(8,128)(2,1)}, u32[]{:S(2)}, u32[]{:S(2)}) async-start(bf16[20,4,32,128]{3,2,0,1:T(8,128)(2,1)} %copy.254), calls=%async_computation.1 | async-start | bytes 1310720 | tf_op jit(solution)/shard_map/all_to_all | solution.py:103
  140.5 496.3 %all-reduce.3.cloned.1.call-start = ((), (), s32[]{:S(2)}) async-start(), calls=%async_computation.6 | async-start | bytes 11796480
  146.2 6.4 copy-start.1
  160.0 4.8 copy-start.2
  236.4 1.1 copy-start.4
  291.2 2.0 copy-start.3
Sparse Core Ops, SparseCore 0:
  291.4 345.4 all-reduce.2
where the time goes:
time: 714 us; the launch traced here: 700 us
  blocking collectives  372 us (52%)
  waiting for transfers between devices  234 us (33%)
  local copies, waits for them, and re-layouts  40.8 us (6%)
  matrix products  21.4 us (3%)
  starting transfers between devices  15.3 us (2%)
  between operations  15.1 us (2%)
    unnamed x2, waiting for transfers between devices  234 us
    all_gather x1, blocking collectives, local(): lax.all_gather(spectral_weight, ('gx', 'gy'), axis=0, tiled=True)  113 us
    psum x1, blocking collectives, local(): mixing_grad = lax.psum(local_mix, ('dp', 'gx', 'gy')) * mix_scale  107 us
    psum x1, blocking collectives, local(): spectral_grad = lax.psum(share, 'dp') * spec_scale  54.8 us
    all_to_all x1, blocking collectives, to_cells(): lax.all_to_all(lax.all_to_all(plane_block, 'gx', split_axis=2, concat_axi...  38.2 us
    all_to_all x1, blocking collectives, to_cells(): lax.all_to_all(plane_block, 'gx', split_axis=2, concat_axis=1, tiled=True)  23.5 us
    all_to_all x1, blocking collectives, to_planes(): lax.all_to_all(lax.all_to_all(block, 'gx', split_axis=1, concat_axis=2, t...  20.1 us
    unnamed x21, local copies, waits for them, and re-layouts  15.6 us
  transfers between devices with their start and end apart: 3, of which 1 were waited for; matrix products, arithmetic and copies ran while one was open for 3% of the time, Pallas kernels for 0%

commit v1 on v0

v1 whole, which is shorter than its diff:
```python
import functools
import math

import jax
import jax.numpy as jnp
import numpy as np
from jax import lax
from jax.experimental import pallas as pl
from jax.experimental.pallas import tpu as pltpu
from jax.sharding import PartitionSpec as P

MESH = pl.DeviceIdType.MESH
F32 = jnp.float32
BF16 = jnp.bfloat16

C = 20
NY = 128
KY = 12
GY = 4
XL = 4
PL_OWN = 4
TILES = 12


def split(table):
    table = np.asarray(table, np.float32)
    hi = table.astype(BF16)
    lo = (table - hi.astype(np.float32)).astype(BF16)
    return np.stack([hi, lo])


@functools.lru_cache(None)
def tables(G):
    nx, kxn = 16 * G, 3 * G
    norm_in = 1.0 / math.sqrt(nx * NY)
    norm_out = 1.0 / math.sqrt(kxn * KY)
    y = np.arange(NY)
    tyf = np.zeros((XL * NY, 128))
    tyi = np.zeros((128, XL * NY))
    for kk in range(3):
        for ks in range(4):
            ang = 2 * np.pi * ((3 * ks + kk) * y % NY) / NY
            for x in range(XL):
                col = kk * 32 + ks * 8 + x * 2
                tyf[x * NY : (x + 1) * NY, col] = np.cos(ang) * norm_in
                tyf[x * NY : (x + 1) * NY, col + 1] = -np.sin(ang) * norm_in
                tyi[col, x * NY : (x + 1) * NY] = np.cos(ang)
                tyi[col + 1, x * NY : (x + 1) * NY] = -np.sin(ang)
    wxp = np.zeros((GY, GY * 6 * G, 32 * G))
    wxi = np.zeros((GY, 32 * G, GY * 8 * G))
    for gy in range(GY):
        for go in range(GY):
            for tri in range(3):
                jj, ks = divmod(3 * go + tri, 4)
                for gq in range(G):
                    j = 3 * gq + jj
                    kx = j if j < kxn // 2 else nx - kxn + j
                    rp = go * 6 * G + gq * 6 + tri * 2
                    ci = go * 8 * G + gq * 8 + tri
                    for gx in range(G):
                        for x in range(XL):
                            ang = 2 * np.pi * (kx * (4 * (gx * GY + gy) + x) % nx) / nx
                            c, s = np.cos(ang), np.sin(ang)
                            k = gx * 32 + ks * 8 + x * 2
                            wxp[gy, rp, k], wxp[gy, rp, k + 1] = c, s
                            wxp[gy, rp + 1, k], wxp[gy, rp + 1, k + 1] = -s, c
                            wxi[gy, k, ci], wxi[gy, k, ci + 4] = c * norm_out, -s * norm_out
                            wxi[gy, k + 1, ci], wxi[gy, k + 1, ci + 4] = s * norm_out, c * norm_out
    px = np.zeros((16 * G, 6 * G))
    pab = np.zeros((3, 16 * G, 32 * G))
    for gq in range(G):
        for ri in range(2):
            for tri in range(3):
                row = gq * 8 + ri * 4 + tri
                px[row, gq * 6 + tri * 2 + ri] = 1
                px[8 * G + row, gq * 6 + tri * 2 + 1 - ri] = 1
                for kk in range(3):
                    src = gq * 32 + kk * 8
                    pab[kk, row, src + tri] = 1
                    pab[kk, 8 * G + row, src + 4 + tri] = -1 if ri == 0 else 1
    selw = np.zeros((32, 18 * 24))
    for kk in range(3):
        for ri in range(2):
            for tri in range(3):
                q = (tri * 3 + kk) * 2 + ri
                selw[kk * 8 + ri * 4 + tri, q * 24 : q * 24 + C] = 1
    lane = np.arange(256)
    ok = lane < 240
    kk, c, i = lane // 80, lane % 80 // 4, lane % 4
    e1 = ((np.arange(24)[:, None] == c[None]) & ok[None]).astype(np.float32)
    same = (kk[:, None] == kk[None]) & (i[:, None] == i[None]) & ok[:, None] & ok[None]
    gmask = np.concatenate([same, same], axis=1).astype(np.float32)
    e2 = np.zeros((512, 128))
    for r in range(2):
        for l in range(240):
            e2[r * 256 + l, r * 60 + kk[l] * 20 + c[l]] = 1
    b = lambda a: np.asarray(a, np.float32).astype(BF16)
    return dict(
        tyf=split(tyf),
        tyi=split(tyi),
        wxp=np.stack([split(w) for w in wxp]),
        wxi=np.stack([split(w) for w in wxi]),
        px=b(px),
        pab=b(pab.reshape(48 * G, 32 * G)),
        selw=b(selw),
        e1=b(e1),
        e2=b(e2),
        gmask=b(gmask),
    )


def mm(a, b):
    return jnp.dot(a, b, preferred_element_type=F32)


def mm_nt(a, b):
    return lax.dot_general(a, b, (((1,), (1,)), ((), ())), preferred_element_type=F32)


def hilo(a):
    hi = a.astype(BF16)
    return hi, (a - hi.astype(F32)).astype(BF16)


def mm_tab(tab, x):
    hi, lo = hilo(x)
    return mm(tab[0], hi) + (mm(tab[0], lo) + mm(tab[1], hi))


def iota(shape, dim):
    return lax.broadcasted_iota(jnp.int32, shape, dim)


def onehot(cond):
    return jnp.where(cond, 1.0, 0.0).astype(BF16)


def gelu_parts(h):
    k = math.sqrt(2.0 / math.pi)
    hh = h * h
    t = jnp.tanh(k * (h + 0.044715 * (hh * h)))
    value = 0.5 * h * (1.0 + t)
    slope = 0.5 * (1.0 + t) + 0.5 * h * (1.0 - t * t) * (k * (1.0 + 3.0 * 0.044715 * hh))
    return value, slope


def kernel(
    G, D, f_ref, mix_ref, w_ref, tyf_ref, px_ref, pab_ref, selw_ref, e1_ref, e2_ref, gmask_ref,
    cot_hbm, tyi_hbm, wxp_hbm, wxi_hbm,
    out_ref, sg_ref, mg_ref,
    cot, tyi, wxp, wxi, a3, mixed, mixpad, backb,
    sx1, rx1, sx3, rx3, sy1, ry1, sy3, ry3, sy2, ry2, sx2, rx2,
    ws, rw, wst, rq, bc, sspec, rspec, sgs, rgs, stt,
    mgx_s, mgx_r, mgy_s, mgy_r, part, rsbuf, agbuf, agsrc,
    lsem, bx_s, bx_r, by_s, by_r, dp_s, dp_r,
):
    rows = C * 4 * G
    planes = 4 * G
    gx = lax.axis_index("gx")
    gy = lax.axis_index("gy")
    dp = lax.axis_index("dp")
    tpr = max(1, -(-TILES // D))
    nred = TILES // tpr

    barrier = pltpu.get_barrier_semaphore()
    for k in range(1, G):
        pl.semaphore_signal(barrier, inc=1, device_id={"gx": lax.rem(gx + k, G)}, device_id_type=MESH)
    for k in range(1, GY):
        pl.semaphore_signal(barrier, inc=1, device_id={"gy": lax.rem(gy + k, GY)}, device_id_type=MESH)
    for k in range(1, D):
        pl.semaphore_signal(barrier, inc=1, device_id={"dp": lax.rem(dp + k, D)}, device_id_type=MESH)

    loads = [
        pltpu.make_async_copy(wxp_hbm.at[gy], wxp, lsem.at[0]),
        pltpu.make_async_copy(cot_hbm, cot, lsem.at[1]),
        pltpu.make_async_copy(tyi_hbm, tyi, lsem.at[2]),
        pltpu.make_async_copy(wxi_hbm.at[gy], wxi, lsem.at[3]),
    ]
    for copy in loads:
        copy.start()

    pending = []

    def exchange(axis, size, me, src_of, dst, sems_s, sems_r, ex):
        def one(k):
            peer = lax.rem(me + k, size)
            return pltpu.make_async_remote_copy(
                src_ref=src_of(peer),
                dst_ref=dst.at[me],
                send_sem=sems_s.at[ex, k],
                recv_sem=sems_r.at[ex, k],
                device_id={axis: peer},
                device_id_type=MESH,
            )

        copies = [one(k) for k in range(1, size)]
        for copy in copies:
            copy.start()
        pending.extend(copies)

        def wait():
            for copy in copies:
                copy.wait_recv()

        return wait

    def ex_x(src_of, dst, ex):
        return exchange("gx", G, gx, src_of, dst, bx_s, bx_r, ex)

    def ex_y(src_of, dst, ex):
        return exchange("gy", GY, gy, src_of, dst, by_s, by_r, ex)

    chunk = min(128, rows)
    starts = list(range(0, rows, chunk))

    def y_forward(data, r0, n):
        a = mm(data, tyf_ref[0]) + mm(data, tyf_ref[1])
        a3[r0 : r0 + n, :] = a
        a3[rows + r0 : rows + r0 + n, :] = pltpu.roll(a, 96, 1)
        a3[2 * rows + r0 : 2 * rows + r0 + n, :] = pltpu.roll(a, 64, 1)

    def to_groups(dst):
        for g in range(G):
            block = a3[pl.ds(g, 240, stride=G), :]
            block = jnp.concatenate([block, jnp.zeros((16, 128), F32)], axis=0)
            dst[g] = block.T[:32]

    for r0 in starts:
        n = min(chunk, rows - r0)
        y_forward(f_ref[r0 : r0 + n, :], r0, n)
    to_groups(sx1)
    pl.semaphore_wait(barrier, G - 1 + GY - 1 + D - 1)
    wait_x1 = ex_x(lambda peer: sx1.at[peer], rx1, 0)
    rx1[gx] = sx1[gx]

    wst[...] = jnp.zeros_like(wst)
    for m in range(9):
        for ri in range(2):
            q = (m * 2 + ri) * 24
            wst[q : q + C, 0:C] = w_ref[m, ri].astype(F32)
    ohd = onehot(iota((128, 640), 0) == (iota((128, 640), 1) & 31))
    wexp = mm(wst[...].astype(BF16), ohd)
    wparts = []
    for q in range(18):
        piece = wexp[q * 24 : q * 24 + 24]
        cond = iota((24, 640), 0) == (iota((24, 640), 1) >> 5)
        wparts.append(jnp.where(cond, piece, 0.0))
    wmasked = jnp.concatenate(wparts, axis=0).astype(BF16)
    ws[...] = mm(selw_ref[...], wmasked).astype(BF16)
    wait_w = ex_x(lambda peer: ws, rw, 1)
    rw[gx] = ws[...]

    mixpad[...] = jnp.zeros_like(mixpad)
    mixpad[0:C, 0:C] = mix_ref[...].astype(F32)
    mixb = mixpad[...].astype(BF16)
    shift = int(math.log2(planes))
    ecol = onehot((iota((128, rows), 1) >> shift) == iota((128, rows), 0))
    for r0 in starts:
        n = min(chunk, rows - r0)
        erow = onehot(((iota((n, 128), 0) + r0) >> shift) == iota((n, 128), 1))
        kron = mm(mm_nt(erow, mixb).astype(BF16), ecol)
        diag = ((iota((n, rows), 0) + r0) & (planes - 1)) == (iota((n, rows), 1) & (planes - 1))
        kron = jnp.where(diag, kron, 0.0).astype(BF16)
        mixed[r0 : r0 + n, :] = mm(kron, f_ref[...])

    for q in range(5):
        lanes = iota((128, 512), 1)
        bc[q] = onehot(iota((128, 512), 0) == ((lanes >> 7) + 4 * q) * 4 + (lanes & 3))
    lanes = iota((128, 512), 1)
    ohr = onehot(iota((128, 512), 0) == (lanes >> 7) * 32 + ((lanes & 127) >> 2))

    def x_forward(recv, send):
        r = recv[...].reshape(32 * G, 256)
        hi, lo = hilo(r)
        p = mm(wxp[0], hi) + (mm(wxp[0], lo) + mm(wxp[1], hi))
        send[...] = p.reshape(GY, 6 * G, 256)

    def y_sum(recv):
        return (recv[0] + recv[1]) + (recv[2] + recv[3])

    loads[0].wait()
    wait_x1()
    x_forward(rx1, sy1)
    wait_y1 = ex_y(lambda peer: sy1.at[peer], ry1, 0)
    ry1[gy] = sy1[gy]

    wait_w()
    rab = mm(pab_ref[...], rw[...].reshape(32 * G, 640)).astype(BF16)
    for q in range(5):
        rq[q] = mm(rab[:, q * 128 : (q + 1) * 128], ohr)

    wait_y1()
    shi, slo = hilo(y_sum(ry1))
    both = mm(px_ref[...], shi) + mm(px_ref[...], slo)
    sspec[...] = both[: 8 * G].reshape(G, 8, 256)

    parts = [both[:, :128]] + [pltpu.roll(both, 256 - 80 * kk, 1)[:, :128] for kk in (1, 2)]
    stacked = jnp.concatenate(parts, axis=0)
    xhi, xlo = hilo(stacked)
    acc = jnp.zeros((48 * G, 128), F32)
    for q in range(5):
        spread = (mm(xhi, bc[q]) + mm(xlo, bc[q])) * rq[q]
        acc += (spread[:, :128] + spread[:, 128:256]) + (spread[:, 256:384] + spread[:, 384:])
    acc = acc.reshape(3, 2, 8 * G, 128)
    acc = acc[:, 0] + acc[:, 1]
    zero = jnp.zeros((8 * G, 128), F32)
    wide = [jnp.concatenate([acc[kk], zero], axis=1) for kk in range(3)]
    vals = wide[0] + pltpu.roll(wide[1], 80, 1) + pltpu.roll(wide[2], 160, 1)
    sy2[...] = vals.astype(BF16)
    wait_y2 = ex_y(lambda peer: sy2, ry2, 1)
    ry2[gy] = sy2[...]

    wait_spec = ex_x(lambda peer: sspec.at[peer], rspec, 2)
    rspec[gx] = sspec[gx]

    loads[3].wait()
    wait_y2()
    v = ry2[...].reshape(32 * G, 256)
    b = mm(wxi[0], v) + mm(wxi[1], v)
    sx2[...] = b.astype(BF16).reshape(G, 32, 256)
    wait_x2 = ex_x(lambda peer: sx2.at[peer], rx2, 3)
    rx2[gx] = sx2[gx]

    wait_spec()
    for tri in range(3):
        s0 = rspec[:, tri : tri + 1, :].reshape(G, 256)
        s1 = rspec[:, 4 + tri : 5 + tri, :].reshape(G, 256)
        block = jnp.concatenate([s0, s1, jnp.zeros((128 - 2 * G, 256), F32)], axis=0)
        stt[tri] = block.T

    loads[1].wait()
    loads[2].wait()
    wait_x2()
    for g in range(G):
        block = rx2[g].astype(F32)
        block = jnp.concatenate([block, jnp.zeros((96, 256), F32)], axis=0)
        a3[pl.ds(g, 240, stride=G), :] = block.T[:240]
    for r0 in starts:
        n = min(chunk, rows - r0)
        bb = a3[r0 : r0 + n, :]
        bb += pltpu.roll(a3[rows + r0 : rows + r0 + n, :], 32, 1)
        bb += pltpu.roll(a3[2 * rows + r0 : 2 * rows + r0 + n, :], 64, 1)
        bb = bb.astype(BF16)
        pre = (mm(bb, tyi[0]) + mm(bb, tyi[1])) + mixed[r0 : r0 + n, :]
        value, slope = gelu_parts(pre)
        out_ref[r0 : r0 + n, :] = value.astype(BF16)
        back = (cot[r0 : r0 + n, :].astype(F32) * slope).astype(BF16)
        backb[r0 : r0 + n, :] = back
        y_forward(back, r0, n)
    to_groups(sx3)
    wait_x3 = ex_x(lambda peer: sx3.at[peer], rx3, 4)
    rx3[gx] = sx3[gx]

    gmix = jnp.zeros((24, 128), F32)
    ecol_t = onehot((iota((rows, 128), 0) >> shift) == iota((rows, 128), 1))
    for r0 in starts:
        n = min(chunk, rows - r0)
        full = mm_nt(f_ref[r0 : r0 + n, :], backb[...])
        diag = ((iota((n, rows), 0) + r0) & (planes - 1)) == (iota((n, rows), 1) & (planes - 1))
        hi, lo = hilo(jnp.where(diag, full, 0.0))
        cols = mm(hi, ecol_t) + mm(lo, ecol_t)
        erow_t = onehot(((iota((24, n), 1) + r0) >> shift) == iota((24, n), 0))
        hi, lo = hilo(cols)
        gmix += mm(erow_t, hi) + mm(erow_t, lo)
    mgx_s[...] = gmix
    wait_mgx = ex_x(lambda peer: mgx_s, mgx_r, 5)
    mgx_r[gx] = gmix

    wait_x3()
    x_forward(rx3, sy3)
    wait_y3 = ex_y(lambda peer: sy3.at[peer], ry3, 2)
    ry3[gy] = sy3[gy]

    wait_mgx()
    total = mgx_r[0]
    for k in range(1, G):
        total += mgx_r[k]
    mgy_s[...] = total
    wait_mgy = ex_y(lambda peer: mgy_s, mgy_r, 3)
    mgy_r[gy] = total

    wait_y3()
    ghi, glo = hilo(y_sum(ry3))
    half = px_ref[0 : 8 * G, :]
    sgs[...] = (mm(half, ghi) + mm(half, glo)).reshape(G, 8, 256)
    wait_gs = ex_x(lambda peer: sgs.at[peer], rgs, 6)
    rgs[gx] = sgs[gx]

    wait_mgy()
    mix_scale = 1.0 / math.sqrt(D * planes * 16 * G * NY)
    part[9:12] = (((mgy_r[0] + mgy_r[1]) + (mgy_r[2] + mgy_r[3])) * mix_scale).reshape(3, 8, 128)

    norm_in = 1.0 / math.sqrt(16 * G * NY)
    norm_out = 1.0 / math.sqrt(36 * G)
    spec_scale = norm_out / norm_in / math.sqrt(D * planes)
    wait_gs()
    gm = gmask_ref[...].astype(F32)
    for tri in range(3):
        g0 = rgs[:, tri : tri + 1, :].reshape(G, 256)
        g1 = rgs[:, 4 + tri : 5 + tri, :].reshape(G, 256)
        top = jnp.concatenate([g0, g1], axis=1)
        bot = jnp.concatenate([g1, -g0], axis=1)
        gg = jnp.concatenate([top, bot, jnp.zeros((128 - 2 * G, 512), F32)], axis=0)
        ahi, alo = hilo(stt[tri])
        bhi, blo = hilo(gg)
        outer = (mm(ahi, bhi) + (mm(ahi, blo) + mm(alo, bhi))) * gm
        ohi, olo = hilo(outer)
        fold = mm(e1_ref[...], ohi) + mm(e1_ref[...], olo)
        fhi, flo = hilo(fold)
        grad = (mm(fhi, e2_ref[...]) + mm(flo, e2_ref[...])) * spec_scale
        part[3 * tri : 3 * tri + 3] = grad.reshape(3, 8, 128)

    def rs_copy(k, to):
        return pltpu.make_async_remote_copy(
            src_ref=part.at[pl.ds(to * tpr, tpr)],
            dst_ref=rsbuf.at[dp],
            send_sem=dp_s.at[0, k],
            recv_sem=dp_r.at[0, k],
            device_id={"dp": to},
            device_id_type=MESH,
        )

    def ag_copy(k, to, slot):
        return pltpu.make_async_remote_copy(
            src_ref=agsrc,
            dst_ref=agbuf.at[slot],
            send_sem=dp_s.at[1, k],
            recv_sem=dp_r.at[1, k],
            device_id={"dp": to},
            device_id_type=MESH,
        )

    for k in range(1, D):
        to = lax.rem(dp + k, D)

        @pl.when(to < nred)
        def _():
            rs_copy(k, to).start()

    @pl.when(dp < nred)
    def _():
        rsbuf[dp] = part[pl.ds(dp * tpr, tpr)]
        for k in range(1, D):
            rs_copy(k, dp).wait_recv()
        tile = rsbuf[0]
        for k in range(1, D):
            tile += rsbuf[k]
        agsrc[...] = tile
        for k in range(1, D):
            ag_copy(k, lax.rem(dp + k, D), dp).start()
        agbuf[dp] = tile

    for k in range(1, D):
        frm = lax.rem(dp + D - k, D)

        @pl.when(frm < nred)
        def _():
            ag_copy(k, dp, frm).wait_recv()

    final = agbuf[...].reshape(TILES, 8, 128)
    mg_ref[...] = final[9:12].reshape(24, 128)[:C, :C]
    for tri in range(3):
        block = final[3 * tri : 3 * tri + 3].reshape(24, 128)
        for kk in range(3):
            for ri in range(2):
                off = ri * 60 + kk * 20
                sg_ref[tri * 3 + kk, ri] = block[:C, off : off + C]

    for copy in pending:
        copy.wait_send()
    for k in range(1, D):
        to = lax.rem(dp + k, D)

        @pl.when(to < nred)
        def _():
            rs_copy(k, to).wait_send()

    @pl.when(dp < nred)
    def _():
        for k in range(1, D):
            ag_copy(k, lax.rem(dp + k, D), dp).wait_send()


def local(G, D, fields, cotangent, mix_weight, spectral_weight):
    rows = C * 4 * G
    cells = XL * NY
    t = tables(G)
    tpr = max(1, -(-TILES // D))
    nred = TILES // tpr
    vm = pl.BlockSpec(memory_space=pltpu.VMEM)
    hbm = pl.BlockSpec(memory_space=pl.ANY)
    V = pltpu.VMEM
    scratch = [
        V((rows, cells), BF16),
        V((2, 128, cells), BF16),
        V((2, GY * 6 * G, 32 * G), BF16),
        V((2, 32 * G, GY * 8 * G), BF16),
        V((3 * rows, 128), F32),
        V((rows, cells), F32),
        V((128, 128), F32),
        V((rows, cells), BF16),
        V((G, 32, 256), F32),
        V((G, 32, 256), F32),
        V((G, 32, 256), F32),
        V((G, 32, 256), F32),
        V((GY, 6 * G, 256), F32),
        V((GY, 6 * G, 256), F32),
        V((GY, 6 * G, 256), F32),
        V((GY, 6 * G, 256), F32),
        V((8 * G, 256), BF16),
        V((GY, 8 * G, 256), BF16),
        V((G, 32, 256), BF16),
        V((G, 32, 256), BF16),
        V((32, 640), BF16),
        V((G, 32, 640), BF16),
        V((432, 128), F32),
        V((5, 48 * G, 512), F32),
        V((5, 128, 512), BF16),
        V((G, 8, 256), F32),
        V((G, 8, 256), F32),
        V((G, 8, 256), F32),
        V((G, 8, 256), F32),
        V((3, 256, 128), F32),
        V((24, 128), F32),
        V((G, 24, 128), F32),
        V((24, 128), F32),
        V((GY, 24, 128), F32),
        V((TILES, 8, 128), F32),
        V((D, tpr, 8, 128), F32),
        V((nred, tpr, 8, 128), F32),
        V((tpr, 8, 128), F32),
        pltpu.SemaphoreType.DMA((4,)),
        pltpu.SemaphoreType.DMA((7, G)),
        pltpu.SemaphoreType.DMA((7, G)),
        pltpu.SemaphoreType.DMA((4, GY)),
        pltpu.SemaphoreType.DMA((4, GY)),
        pltpu.SemaphoreType.DMA((2, D)),
        pltpu.SemaphoreType.DMA((2, D)),
    ]
    out, sg, mg = pl.pallas_call(
        functools.partial(kernel, G, D),
        out_shape=(
            jax.ShapeDtypeStruct((rows, cells), BF16),
            jax.ShapeDtypeStruct((9, 2, C, C), F32),
            jax.ShapeDtypeStruct((C, C), F32),
        ),
        in_specs=[vm] * 10 + [hbm] * 4,
        out_specs=(vm, vm, vm),
        scratch_shapes=scratch,
        compiler_params=pltpu.CompilerParams(
            collective_id=0, has_side_effects=True, vmem_limit_bytes=60 * 1024 * 1024
        ),
    )(
        fields.reshape(rows, cells),
        mix_weight,
        spectral_weight,
        t["tyf"],
        t["px"],
        t["pab"],
        t["selw"],
        t["e1"],
        t["e2"],
        t["gmask"],
        cotangent.reshape(rows, cells),
        t["tyi"],
        t["wxp"],
        t["wxi"],
    )
    return out.reshape(fields.shape), sg, mg


def solution(mesh):
    G, D = mesh.shape["gx"], mesh.shape["dp"]
    cells = P("dp", None, None, ("gx", "gy"))
    modes = P(("gx", "gy"), None, None, None)
    return jax.shard_map(
        functools.partial(local, G, D),
        mesh=mesh,
        in_specs=(cells, cells, P(), modes),
        out_specs=(cells, modes, P()),
        check_vma=False,
    )
```

time: 714 us -> 81.6 us (0.11); the launches traced: 700 us -> 81.4 us
  blocking collectives: 372 us -> 0 us
  waiting for transfers between devices: 234 us -> 0 us
  Pallas kernels: 0 us -> 74.9 us
  local copies, waits for them, and re-layouts: 40.8 us -> 5.86 us
  matrix products: 21.4 us -> 0 us
  starting transfers between devices: 15.3 us -> 0 us
  between operations: 15.1 us -> 0.64 us
    unnamed x2 -> x0, waiting for transfers between devices: 234 us -> none
    psum x2 -> x0, blocking collectives: 162 us -> none  [the longest x1 107 us: local(): mixing_grad = lax.psum(local_mix, ('dp', 'gx', 'gy')) * mix_scale]
    all_gather x1 -> x0, blocking collectives: 113 us -> none  [local(): lax.all_gather(spectral_weight, ('gx', 'gy'), axis=0, tiled=True)]
    all_to_all x4 -> x0, blocking collectives: 97.3 us -> none  [the longest x1 38.2 us: to_cells(): lax.all_to_all(lax.all_to_all(plane_block, 'gx', split_axis=2, concat_axi...]
    pallas_call x0 -> x1, Pallas kernels: none -> 74.9 us  [local(): pl.pallas_call(functools.partial(kernel, G, D), out_shape=(jax.ShapeDtype...]
    dot_general x20 -> x0, matrix products: 21.4 us -> none  [the longest x1 4.7 us: local(): jnp.einsum('cpq,cd->dpq', flat, mix_weight, preferred_element_type=jnp.fl...]
    all_to_all x2 -> x0, starting transfers between devices: 15.3 us -> none  [the longest x1 10.9 us: to_planes(): lax.all_to_all(block, 'gx', split_axis=1, concat_axis=2, tiled=True)]
    another operation x12 -> x0, local copies, waits for them, and re-layouts: 10.7 us -> none  [the longest x1 6.05 us: grads_of(): return jnp.stack([g_re, g_im], axis=1)]
  transfers between devices with their start and end apart: 3 -> 0, of which waited for: 1 -> 0; matrix products, arithmetic and copies ran while one was open for 3% -> 0% of each run, Pallas kernels for 0% -> 0%
where the time goes in v1:
time: 81.6 us; the launch traced here: 81.4 us
  Pallas kernels  74.9 us (92%)
  local copies, waits for them, and re-layouts  5.86 us (7%)
    pallas_call x1, Pallas kernels, local(): pl.pallas_call(functools.partial(kernel, G, D), out_shape=(jax.ShapeDtype...  74.9 us
    unnamed x6, local copies, waits for them, and re-layouts  5.86 us

profile of v1, /device:TPU:1, one launch (start us, length us, event | category | flops | bytes accessed | tf_op | source)
XLA Modules:
  0.0 81.4 jit_solution(5889123848817644487)
XLA Ops:
  0.6 1.6 %copy.17.w_ref = bf16[9,2,20,20]{3,2,1,0:T(8,128)(2,1)} copy(bf16[9,2,20,20]{3,1,2,0:T(2,128)(2,1)} %param.17) | data formatting | bytes 28800 | tf_op args[3]
  2.2 74.9 %shard_map.157 = (bf16[640,512]{1,0:T(8,128)(2,1)}, f32[9,2,20,20]{3,2,1,0:T(8,128)}, f32[20,20]{1,0:T(8,128)}) custom-call(bf16[640,512]{1,0:T(8,128)(2,1)} %bitcast.3, bf16[20,20]{1,0:T(8,128)(2,1)} %mix_ref.1, bf16[9,2,20,20]{3,2,1,0:T(8,128)(2,1)} %copy.17.w_ref, bf16[2,512,128]{2,1,0:T(8,128)(2,1)} %constant.20.clone.tyf_ref, ...), custom_call_target="tpu_custom_call" | custom-call | tf_op jit(solution)/shard_map/pallas_call | solution.py:540
  77.1 1.7 %copy.18 = f32[9,2,20,20]{3,1,2,0:T(2,128)} copy(f32[9,2,20,20]{3,2,1,0:T(8,128)} %get-tuple-element.10) | data formatting | bytes 57600
  78.8 0.0 copy-start
  78.8 2.0 %copy.21 = bf16[1,20,32,512]{3,2,1,0:T(8,128)(2,1)} copy(bf16[1,20,32,512]{3,2,1,0:T(8,128)(2,1)} %bitcast.5) | data formatting | bytes 1310720
  80.8 0.0 copy-done
  80.8 0.6 copy.22
Async XLA Ops:
  78.8 2.0 %copy-start = (f32[20,20]{1,0:T(8,128)S(1)}, f32[20,20]{1,0:T(8,128)}, u32[]{:S(2)}) copy-start(f32[20,20]{1,0:T(8,128)} %get-tuple-element.17) | copy-start | bytes 4804

commit v2 on v1

--- a/solution.py
+++ b/solution.py
@@ -82,17 +82,15 @@
     for kk in range(3):
         for ri in range(2):
             for tri in range(3):
-                q = (tri * 3 + kk) * 2 + ri
-                selw[kk * 8 + ri * 4 + tri, q * 24 : q * 24 + C] = 1
+                q = (tri * 3 + kk) * 48 + ri
+                selw[kk * 8 + ri * 4 + tri, q : q + 2 * C : 2] = 1
     lane = np.arange(256)
-    ok = lane < 240
-    kk, c, i = lane // 80, lane % 80 // 4, lane % 4
+    ok = lane % 128 < 120
+    kk, c = lane % 128 // 40, lane // 128 * 10 + lane % 128 % 40 // 4
     e1 = ((np.arange(24)[:, None] == c[None]) & ok[None]).astype(np.float32)
-    same = (kk[:, None] == kk[None]) & (i[:, None] == i[None]) & ok[:, None] & ok[None]
-    gmask = np.concatenate([same, same], axis=1).astype(np.float32)
     e2 = np.zeros((512, 128))
     for r in range(2):
-        for l in range(240):
+        for l in lane[ok]:
             e2[r * 256 + l, r * 60 + kk[l] * 20 + c[l]] = 1
     b = lambda a: np.asarray(a, np.float32).astype(BF16)
     return dict(
@@ -105,7 +103,6 @@
         selw=b(selw),
         e1=b(e1),
         e2=b(e2),
-        gmask=b(gmask),
     )
 
 
@@ -133,6 +130,11 @@
 
 def onehot(cond):
     return jnp.where(cond, 1.0, 0.0).astype(BF16)
+
+
+def key(lane):
+    r = lane & 127
+    return jnp.where(r >= 80, 8, jnp.where(r >= 40, 4, 0)) + (lane & 3)
 
 
 def gelu_parts(h):
@@ -145,7 +147,7 @@
 
 
 def kernel(
-    G, D, f_ref, mix_ref, w_ref, tyf_ref, px_ref, pab_ref, selw_ref, e1_ref, e2_ref, gmask_ref,
+    G, D, f_ref, mix_ref, w_ref, tyf_ref, px_ref, pab_ref, selw_ref, e1_ref, e2_ref,
     cot_hbm, tyi_hbm, wxp_hbm, wxi_hbm,
     out_ref, sg_ref, mg_ref,
     cot, tyi, wxp, wxi, a3, mixed, mixpad, backb,
@@ -210,53 +212,53 @@
     def ex_y(src_of, dst, ex):
         return exchange("gy", GY, gy, src_of, dst, by_s, by_r, ex)
 
-    chunk = min(128, rows)
-    starts = list(range(0, rows, chunk))
-
-    def y_forward(data, r0, n):
+    hrows = rows // 2
+    chunk = 160 if hrows % 160 == 0 else hrows
+    chunks = [[h * hrows + r for r in range(0, hrows, chunk)] for h in range(2)]
+    starts = chunks[0] + chunks[1]
+    n = chunk
+    rest = jnp.zeros((8, 128), F32)
+
+    def part_of(h, kk, r0):
+        return pl.ds((h * 3 + kk) * hrows + r0 - h * hrows, n)
+
+    def y_forward(data, h, r0):
         a = mm(data, tyf_ref[0]) + mm(data, tyf_ref[1])
-        a3[r0 : r0 + n, :] = a
-        a3[rows + r0 : rows + r0 + n, :] = pltpu.roll(a, 96, 1)
-        a3[2 * rows + r0 : 2 * rows + r0 + n, :] = pltpu.roll(a, 64, 1)
-
-    def to_groups(dst):
+        a3[part_of(h, 0, r0), :] = a
+        a3[part_of(h, 1, r0), :] = pltpu.roll(a, 96, 1)
+        a3[part_of(h, 2, r0), :] = pltpu.roll(a, 64, 1)
+
+    def to_groups(h, dst):
         for g in range(G):
-            block = a3[pl.ds(g, 240, stride=G), :]
-            block = jnp.concatenate([block, jnp.zeros((16, 128), F32)], axis=0)
-            dst[g] = block.T[:32]
-
-    for r0 in starts:
-        n = min(chunk, rows - r0)
-        y_forward(f_ref[r0 : r0 + n, :], r0, n)
-    to_groups(sx1)
+            block = a3[pl.ds(h * 3 * hrows + g, 120, stride=G), :]
+            dst[h, g] = jnp.concatenate([block, rest], axis=0).T[:32]
+
+    for h in range(2):
+        for r0 in chunks[h]:
+            y_forward(f_ref[r0 : r0 + n, :], h, r0)
+        to_groups(h, sx1)
     pl.semaphore_wait(barrier, G - 1 + GY - 1 + D - 1)
-    wait_x1 = ex_x(lambda peer: sx1.at[peer], rx1, 0)
-    rx1[gx] = sx1[gx]
+    wait_x1 = [ex_x(lambda peer: sx1.at[h, peer], rx1.at[h], h) for h in range(2)]
+    for h in range(2):
+        rx1[h, gx] = sx1[h, gx]
 
     wst[...] = jnp.zeros_like(wst)
     for m in range(9):
-        for ri in range(2):
-            q = (m * 2 + ri) * 24
-            wst[q : q + C, 0:C] = w_ref[m, ri].astype(F32)
+        wst[m * 48 : m * 48 + 2 * C, 0:C] = w_ref[m].astype(F32).reshape(2 * C, C)
     ohd = onehot(iota((128, 640), 0) == (iota((128, 640), 1) & 31))
     wexp = mm(wst[...].astype(BF16), ohd)
     wparts = []
-    for q in range(18):
-        piece = wexp[q * 24 : q * 24 + 24]
-        cond = iota((24, 640), 0) == (iota((24, 640), 1) >> 5)
-        wparts.append(jnp.where(cond, piece, 0.0))
+    for m in range(9):
+        cond = (iota((48, 640), 0) >> 1) == (iota((48, 640), 1) >> 5)
+        wparts.append(jnp.where(cond, wexp[m * 48 : m * 48 + 48], 0.0))
     wmasked = jnp.concatenate(wparts, axis=0).astype(BF16)
     ws[...] = mm(selw_ref[...], wmasked).astype(BF16)
-    wait_w = ex_x(lambda peer: ws, rw, 1)
-    rw[gx] = ws[...]
-
     mixpad[...] = jnp.zeros_like(mixpad)
     mixpad[0:C, 0:C] = mix_ref[...].astype(F32)
     mixb = mixpad[...].astype(BF16)
     shift = int(math.log2(planes))
     ecol = onehot((iota((128, rows), 1) >> shift) == iota((128, rows), 0))
     for r0 in starts:
-        n = min(chunk, rows - r0)
         erow = onehot(((iota((n, 128), 0) + r0) >> shift) == iota((n, 128), 1))
         kron = mm(mm_nt(erow, mixb).astype(BF16), ecol)
         diag = ((iota((n, rows), 0) + r0) & (planes - 1)) == (iota((n, rows), 1) & (planes - 1))
@@ -269,32 +271,42 @@
     lanes = iota((128, 512), 1)
     ohr = onehot(iota((128, 512), 0) == (lanes >> 7) * 32 + ((lanes & 127) >> 2))
 
-    def x_forward(recv, send):
-        r = recv[...].reshape(32 * G, 256)
-        hi, lo = hilo(r)
+    def x_forward(recv, send, h):
+        hi, lo = hilo(recv[h].reshape(32 * G, 128))
         p = mm(wxp[0], hi) + (mm(wxp[0], lo) + mm(wxp[1], hi))
-        send[...] = p.reshape(GY, 6 * G, 256)
+        send[h] = p.reshape(GY, 6 * G, 128)
 
     def y_sum(recv):
-        return (recv[0] + recv[1]) + (recv[2] + recv[3])
+        halves = [(recv[h, 0] + recv[h, 1]) + (recv[h, 2] + recv[h, 3]) for h in range(2)]
+        return jnp.concatenate(halves, axis=1)
 
     loads[0].wait()
-    wait_x1()
-    x_forward(rx1, sy1)
-    wait_y1 = ex_y(lambda peer: sy1.at[peer], ry1, 0)
-    ry1[gy] = sy1[gy]
+    wait_y1 = []
+    for h in range(2):
+        wait_x1[h]()
+        x_forward(rx1, sy1, h)
+        wait_y1.append(ex_y(lambda peer: sy1.at[h, peer], ry1.at[h], h))
+        ry1[h, gy] = sy1[h, gy]
+    wait_w = ex_x(lambda peer: ws, rw, 2)
+    rw[gx] = ws[...]
 
     wait_w()
     rab = mm(pab_ref[...], rw[...].reshape(32 * G, 640)).astype(BF16)
     for q in range(5):
         rq[q] = mm(rab[:, q * 128 : (q + 1) * 128], ohr)
 
-    wait_y1()
+    for h in range(2):
+        wait_y1[h]()
     shi, slo = hilo(y_sum(ry1))
     both = mm(px_ref[...], shi) + mm(px_ref[...], slo)
     sspec[...] = both[: 8 * G].reshape(G, 8, 256)
 
-    parts = [both[:, :128]] + [pltpu.roll(both, 256 - 80 * kk, 1)[:, :128] for kk in (1, 2)]
+    low = iota((16 * G, 128), 1) < 40
+    turn = lambda a, by: pltpu.roll(a, by % 128, 1) if by % 128 else a
+    parts = []
+    for kk in range(3):
+        h0, h1 = turn(both[:, :128], -40 * kk), turn(both[:, 128:], 40 - 40 * kk)
+        parts.append(jnp.where(low, h0, h1))
     stacked = jnp.concatenate(parts, axis=0)
     xhi, xlo = hilo(stacked)
     acc = jnp.zeros((48 * G, 128), F32)
@@ -303,23 +315,27 @@
         acc += (spread[:, :128] + spread[:, 128:256]) + (spread[:, 256:384] + spread[:, 384:])
     acc = acc.reshape(3, 2, 8 * G, 128)
     acc = acc[:, 0] + acc[:, 1]
-    zero = jnp.zeros((8 * G, 128), F32)
-    wide = [jnp.concatenate([acc[kk], zero], axis=1) for kk in range(3)]
-    vals = wide[0] + pltpu.roll(wide[1], 80, 1) + pltpu.roll(wide[2], 160, 1)
-    sy2[...] = vals.astype(BF16)
-    wait_y2 = ex_y(lambda peer: sy2, ry2, 1)
-    ry2[gy] = sy2[...]
-
-    wait_spec = ex_x(lambda peer: sspec.at[peer], rspec, 2)
+    low = low[: 8 * G]
+    wait_y2 = []
+    for h in range(2):
+        mine = [jnp.where(low if h == 0 else ~low, acc[kk], 0.0) for kk in range(3)]
+        vals = sum(turn(mine[kk], 40 * kk - 40 * h) for kk in range(3))
+        sy2[h] = vals.astype(BF16)
+        wait_y2.append(ex_y(lambda peer: sy2.at[h], ry2.at[h], 2 + h))
+        ry2[h, gy] = sy2[h]
+
+    wait_spec = ex_x(lambda peer: sspec.at[peer], rspec, 3)
     rspec[gx] = sspec[gx]
 
     loads[3].wait()
-    wait_y2()
-    v = ry2[...].reshape(32 * G, 256)
-    b = mm(wxi[0], v) + mm(wxi[1], v)
-    sx2[...] = b.astype(BF16).reshape(G, 32, 256)
-    wait_x2 = ex_x(lambda peer: sx2.at[peer], rx2, 3)
-    rx2[gx] = sx2[gx]
+    wait_x2 = []
+    for h in range(2):
+        wait_y2[h]()
+        v = ry2[h].reshape(32 * G, 128)
+        b = mm(wxi[0], v) + mm(wxi[1], v)
+        sx2[h] = b.astype(BF16).reshape(G, 32, 128)
+        wait_x2.append(ex_x(lambda peer: sx2.at[h, peer], rx2.at[h], 4 + h))
+        rx2[h, gx] = sx2[h, gx]
 
     wait_spec()
     for tri in range(3):
@@ -330,31 +346,30 @@
 
     loads[1].wait()
     loads[2].wait()
-    wait_x2()
-    for g in range(G):
-        block = rx2[g].astype(F32)
-        block = jnp.concatenate([block, jnp.zeros((96, 256), F32)], axis=0)
-        a3[pl.ds(g, 240, stride=G), :] = block.T[:240]
-    for r0 in starts:
-        n = min(chunk, rows - r0)
-        bb = a3[r0 : r0 + n, :]
-        bb += pltpu.roll(a3[rows + r0 : rows + r0 + n, :], 32, 1)
-        bb += pltpu.roll(a3[2 * rows + r0 : 2 * rows + r0 + n, :], 64, 1)
-        bb = bb.astype(BF16)
-        pre = (mm(bb, tyi[0]) + mm(bb, tyi[1])) + mixed[r0 : r0 + n, :]
-        value, slope = gelu_parts(pre)
-        out_ref[r0 : r0 + n, :] = value.astype(BF16)
-        back = (cot[r0 : r0 + n, :].astype(F32) * slope).astype(BF16)
-        backb[r0 : r0 + n, :] = back
-        y_forward(back, r0, n)
-    to_groups(sx3)
-    wait_x3 = ex_x(lambda peer: sx3.at[peer], rx3, 4)
-    rx3[gx] = sx3[gx]
+    wait_x3 = []
+    for h in range(2):
+        wait_x2[h]()
+        for g in range(G):
+            block = jnp.concatenate([rx2[h, g].astype(F32), jnp.zeros((96, 128), F32)], axis=0)
+            a3[pl.ds(h * 3 * hrows + g, 120, stride=G), :] = block.T[:120]
+        for r0 in chunks[h]:
+            bb = a3[part_of(h, 0, r0), :]
+            bb += pltpu.roll(a3[part_of(h, 1, r0), :], 32, 1)
+            bb += pltpu.roll(a3[part_of(h, 2, r0), :], 64, 1)
+            bb = bb.astype(BF16)
+            pre = (mm(bb, tyi[0]) + mm(bb, tyi[1])) + mixed[r0 : r0 + n, :]
+            value, slope = gelu_parts(pre)
+            out_ref[r0 : r0 + n, :] = value.astype(BF16)
+            back = (cot[r0 : r0 + n, :].astype(F32) * slope).astype(BF16)
+            backb[r0 : r0 + n, :] = back
+            y_forward(back, h, r0)
+        to_groups(h, sx3)
+        wait_x3.append(ex_x(lambda peer: sx3.at[h, peer], rx3.at[h], 6 + h))
+        rx3[h, gx] = sx3[h, gx]
 
     gmix = jnp.zeros((24, 128), F32)
     ecol_t = onehot((iota((rows, 128), 0) >> shift) == iota((rows, 128), 1))
     for r0 in starts:
-        n = min(chunk, rows - r0)
         full = mm_nt(f_ref[r0 : r0 + n, :], backb[...])
         diag = ((iota((n, rows), 0) + r0) & (planes - 1)) == (iota((n, rows), 1) & (planes - 1))
         hi, lo = hilo(jnp.where(diag, full, 0.0))
@@ -363,27 +378,30 @@
         hi, lo = hilo(cols)
         gmix += mm(erow_t, hi) + mm(erow_t, lo)
     mgx_s[...] = gmix
-    wait_mgx = ex_x(lambda peer: mgx_s, mgx_r, 5)
+    wait_mgx = ex_x(lambda peer: mgx_s, mgx_r, 8)
     mgx_r[gx] = gmix
 
-    wait_x3()
-    x_forward(rx3, sy3)
-    wait_y3 = ex_y(lambda peer: sy3.at[peer], ry3, 2)
-    ry3[gy] = sy3[gy]
+    wait_y3 = []
+    for h in range(2):
+        wait_x3[h]()
+        x_forward(rx3, sy3, h)
+        wait_y3.append(ex_y(lambda peer: sy3.at[h, peer], ry3.at[h], 4 + h))
+        ry3[h, gy] = sy3[h, gy]
 
     wait_mgx()
     total = mgx_r[0]
     for k in range(1, G):
         total += mgx_r[k]
     mgy_s[...] = total
-    wait_mgy = ex_y(lambda peer: mgy_s, mgy_r, 3)
+    wait_mgy = ex_y(lambda peer: mgy_s, mgy_r, 6)
     mgy_r[gy] = total
 
-    wait_y3()
+    for h in range(2):
+        wait_y3[h]()
     ghi, glo = hilo(y_sum(ry3))
     half = px_ref[0 : 8 * G, :]
     sgs[...] = (mm(half, ghi) + mm(half, glo)).reshape(G, 8, 256)
-    wait_gs = ex_x(lambda peer: sgs.at[peer], rgs, 6)
+    wait_gs = ex_x(lambda peer: sgs.at[peer], rgs, 9)
     rgs[gx] = sgs[gx]
 
     wait_mgy()
@@ -394,7 +412,7 @@
     norm_out = 1.0 / math.sqrt(36 * G)
     spec_scale = norm_out / norm_in / math.sqrt(D * planes)
     wait_gs()
-    gm = gmask_ref[...].astype(F32)
+    gm = key(iota((256, 512), 0)) == key(iota((256, 512), 1) & 255)
     for tri in range(3):
         g0 = rgs[:, tri : tri + 1, :].reshape(G, 256)
         g1 = rgs[:, 4 + tri : 5 + tri, :].reshape(G, 256)
@@ -403,7 +421,8 @@
         gg = jnp.concatenate([top, bot, jnp.zeros((128 - 2 * G, 512), F32)], axis=0)
         ahi, alo = hilo(stt[tri])
         bhi, blo = hilo(gg)
-        outer = (mm(ahi, bhi) + (mm(ahi, blo) + mm(alo, bhi))) * gm
+        outer = (mm(ahi, bhi) + (mm(ahi, blo) + mm(alo, bhi)))
+        outer = jnp.where(gm, outer, 0.0)
         ohi, olo = hilo(outer)
         fold = mm(e1_ref[...], ohi) + mm(e1_ref[...], olo)
         fhi, flo = hilo(fold)
@@ -464,7 +483,7 @@
         for kk in range(3):
             for ri in range(2):
                 off = ri * 60 + kk * 20
-                sg_ref[tri * 3 + kk, ri] = block[:C, off : off + C]
+                sg_ref[tri * 3 + kk, :, ri, :] = block[:C, off : off + C]
 
     for copy in pending:
         copy.wait_send()
@@ -499,18 +518,18 @@
         V((rows, cells), F32),
         V((128, 128), F32),
         V((rows, cells), BF16),
-        V((G, 32, 256), F32),
-        V((G, 32, 256), F32),
-        V((G, 32, 256), F32),
-        V((G, 32, 256), F32),
-        V((GY, 6 * G, 256), F32),
-        V((GY, 6 * G, 256), F32),
-        V((GY, 6 * G, 256), F32),
-        V((GY, 6 * G, 256), F32),
-        V((8 * G, 256), BF16),
-        V((GY, 8 * G, 256), BF16),
-        V((G, 32, 256), BF16),
-        V((G, 32, 256), BF16),
+        V((2, G, 32, 128), F32),
+        V((2, G, 32, 128), F32),
+        V((2, G, 32, 128), F32),
+        V((2, G, 32, 128), F32),
+        V((2, GY, 6 * G, 128), F32),
+        V((2, GY, 6 * G, 128), F32),
+        V((2, GY, 6 * G, 128), F32),
+        V((2, GY, 6 * G, 128), F32),
+        V((2, 8 * G, 128), BF16),
+        V((2, GY, 8 * G, 128), BF16),
+        V((2, G, 32, 128), BF16),
+        V((2, G, 32, 128), BF16),
         V((32, 640), BF16),
         V((G, 32, 640), BF16),
         V((432, 128), F32),
@@ -530,21 +549,21 @@
         V((nred, tpr, 8, 128), F32),
         V((tpr, 8, 128), F32),
         pltpu.SemaphoreType.DMA((4,)),
-        pltpu.SemaphoreType.DMA((7, G)),
-        pltpu.SemaphoreType.DMA((7, G)),
-        pltpu.SemaphoreType.DMA((4, GY)),
-        pltpu.SemaphoreType.DMA((4, GY)),
+        pltpu.SemaphoreType.DMA((10, G)),
+        pltpu.SemaphoreType.DMA((10, G)),
+        pltpu.SemaphoreType.DMA((7, GY)),
+        pltpu.SemaphoreType.DMA((7, GY)),
         pltpu.SemaphoreType.DMA((2, D)),
         pltpu.SemaphoreType.DMA((2, D)),
     ]
     out, sg, mg = pl.pallas_call(
         functools.partial(kernel, G, D),
         out_shape=(
-            jax.ShapeDtypeStruct((rows, cells), BF16),
-            jax.ShapeDtypeStruct((9, 2, C, C), F32),
-            jax.ShapeDtypeStruct((C, C), F32),
+            V((rows, cells), BF16),
+            V((9, C, 2, C), F32),
+            V((C, C), F32),
         ),
-        in_specs=[vm] * 10 + [hbm] * 4,
+        in_specs=[vm] * 9 + [hbm] * 4,
         out_specs=(vm, vm, vm),
         scratch_shapes=scratch,
         compiler_params=pltpu.CompilerParams(
@@ -553,20 +572,19 @@
     )(
         fields.reshape(rows, cells),
         mix_weight,
-        spectral_weight,
+        spectral_weight.transpose(0, 2, 1, 3),
         t["tyf"],
         t["px"],
         t["pab"],
         t["selw"],
         t["e1"],
         t["e2"],
-        t["gmask"],
         cotangent.reshape(rows, cells),
         t["tyi"],
         t["wxp"],
         t["wxi"],
     )
-    return out.reshape(fields.shape), sg, mg
+    return out.reshape(fields.shape), sg.transpose(0, 2, 1, 3), mg
 
 
 def solution(mesh):

time: 81.6 us -> 74 us (0.907)
  Pallas kernels: 74.9 us -> 71.1 us
  local copies, waits for them, and re-layouts: 5.86 us -> 2.11 us
    pallas_call x1, Pallas kernels: 74.9 us -> 71.1 us  [local(): pl.pallas_call(functools.partial(kernel, G, D), out_shape=(V((rows, cells...]
    unnamed x6 -> x3, local copies, waits for them, and re-layouts: 5.86 us -> 2.11 us
where the time goes in v2:
time: 74 us; the launch traced here: 73.8 us
  Pallas kernels  71.1 us (96%)
  local copies, waits for them, and re-layouts  2.11 us (3%)
    pallas_call x1, Pallas kernels, local(): pl.pallas_call(functools.partial(kernel, G, D), out_shape=(V((rows, cells...  71.1 us
    unnamed x3, local copies, waits for them, and re-layouts  2.11 us

profile of v2, /device:TPU:1, one launch (start us, length us, event | category | flops | bytes accessed | tf_op | source)
XLA Modules:
  0.0 73.8 jit_solution(12254820280850869612)
XLA Ops:
  0.6 71.1 %shard_map.148 = (bf16[640,512]{1,0:T(8,128)(2,1)S(1)}, f32[9,20,2,20]{3,2,1,0:T(2,128)S(1)}, f32[20,20]{1,0:T(8,128)S(1)}) custom-call(bf16[640,512]{1,0:T(8,128)(2,1)} %bitcast.7, bf16[20,20]{1,0:T(8,128)(2,1)} %mix_ref.1, bf16[9,20,2,20]{3,2,1,0:T(2,128)(2,1)} %bitcast.9, bf16[2,512,128]{2,1,0:T(8,128)(2,1)} %constant.18.clone.tyf_ref, ...), custom_call_target="tpu_custom_call" | custom-call | tf_op jit(solution)/shard_map/pallas_call | solution.py:559
  71.7 0.8 %copy.19 = bf16[1,20,32,512]{3,2,1,0:T(8,128)(2,1)} copy(bf16[1,20,32,512]{3,2,1,0:T(8,128)(2,1)S(1)} %bitcast.5) | data formatting | bytes 1310720
  72.5 0.7 copy.20
  73.2 0.6 copy.21

commit v3 on v2

--- a/solution.py
+++ b/solution.py
@@ -66,32 +66,23 @@
                             wxp[gy, rp + 1, k], wxp[gy, rp + 1, k + 1] = -s, c
                             wxi[gy, k, ci], wxi[gy, k, ci + 4] = c * norm_out, -s * norm_out
                             wxi[gy, k + 1, ci], wxi[gy, k + 1, ci + 4] = s * norm_out, c * norm_out
-    px = np.zeros((16 * G, 6 * G))
-    pab = np.zeros((3, 16 * G, 32 * G))
+    px = np.zeros((8 * G, 6 * G))
+    pab = np.zeros((2, 3, 8 * G, 32 * G))
     for gq in range(G):
         for ri in range(2):
             for tri in range(3):
                 row = gq * 8 + ri * 4 + tri
                 px[row, gq * 6 + tri * 2 + ri] = 1
-                px[8 * G + row, gq * 6 + tri * 2 + 1 - ri] = 1
                 for kk in range(3):
                     src = gq * 32 + kk * 8
-                    pab[kk, row, src + tri] = 1
-                    pab[kk, 8 * G + row, src + 4 + tri] = -1 if ri == 0 else 1
+                    pab[0, kk, row, src + tri] = 1
+                    pab[1, kk, row, src + 4 + tri] = 1 if ri == 0 else -1
     selw = np.zeros((32, 18 * 24))
     for kk in range(3):
         for ri in range(2):
             for tri in range(3):
                 q = (tri * 3 + kk) * 48 + ri
                 selw[kk * 8 + ri * 4 + tri, q : q + 2 * C : 2] = 1
-    lane = np.arange(256)
-    ok = lane % 128 < 120
-    kk, c = lane % 128 // 40, lane // 128 * 10 + lane % 128 % 40 // 4
-    e1 = ((np.arange(24)[:, None] == c[None]) & ok[None]).astype(np.float32)
-    e2 = np.zeros((512, 128))
-    for r in range(2):
-        for l in lane[ok]:
-            e2[r * 256 + l, r * 60 + kk[l] * 20 + c[l]] = 1
     b = lambda a: np.asarray(a, np.float32).astype(BF16)
     return dict(
         tyf=split(tyf),
@@ -101,8 +92,6 @@
         px=b(px),
         pab=b(pab.reshape(48 * G, 32 * G)),
         selw=b(selw),
-        e1=b(e1),
-        e2=b(e2),
     )
 
 
@@ -132,9 +121,12 @@
     return jnp.where(cond, 1.0, 0.0).astype(BF16)
 
 
-def key(lane):
-    r = lane & 127
-    return jnp.where(r >= 80, 8, jnp.where(r >= 40, 4, 0)) + (lane & 3)
+def lane_code(shape, stride):
+    row = iota(shape, 0)
+    q = row & 127
+    kk = jnp.where(q >= 80, 2, jnp.where(q >= 40, 1, 0))
+    c = (row >> 7) * 10 + ((q - 40 * kk) >> 2)
+    return jnp.where(q < 120, (kk * stride + c) * 4 + (q & 3), -1)
 
 
 def gelu_parts(h):
@@ -147,12 +139,11 @@
 
 
 def kernel(
-    G, D, f_ref, mix_ref, w_ref, tyf_ref, px_ref, pab_ref, selw_ref, e1_ref, e2_ref,
-    cot_hbm, tyi_hbm, wxp_hbm, wxi_hbm,
+    G, D, f_hbm, tyf_hbm, w_hbm, mix_hbm, selw_hbm, wxp_hbm, pab_hbm, px_hbm, wxi_hbm, cot_hbm, tyi_hbm,
     out_ref, sg_ref, mg_ref,
-    cot, tyi, wxp, wxi, a3, mixed, mixpad, backb,
+    f_ref, tyf_ref, w_ref, mix_ref, selw_ref, wxp, pab_ref, px_ref, wxi, cot, tyi, a3, mixed, mixpad, backb,
     sx1, rx1, sx3, rx3, sy1, ry1, sy3, ry3, sy2, ry2, sx2, rx2,
-    ws, rw, wst, rq, bc, sspec, rspec, sgs, rgs, stt,
+    ws, rw, wst, rq, bc, ohg, gi, sspec, rspec, sgs, rgs, stt,
     mgx_s, mgx_r, mgy_s, mgy_r, part, rsbuf, agbuf, agsrc,
     lsem, bx_s, bx_r, by_s, by_r, dp_s, dp_r,
 ):
@@ -164,6 +155,11 @@
     tpr = max(1, -(-TILES // D))
     nred = TILES // tpr
 
+    hrows = rows // 2
+    chunk = 160 if hrows % 160 == 0 else hrows
+    chunks = [[h * hrows + r for r in range(0, hrows, chunk)] for h in range(2)]
+    starts = chunks[0] + chunks[1]
+    n = chunk
     barrier = pltpu.get_barrier_semaphore()
     for k in range(1, G):
         pl.semaphore_signal(barrier, inc=1, device_id={"gx": lax.rem(gx + k, G)}, device_id_type=MESH)
@@ -172,14 +168,14 @@
     for k in range(1, D):
         pl.semaphore_signal(barrier, inc=1, device_id={"dp": lax.rem(dp + k, D)}, device_id_type=MESH)
 
-    loads = [
-        pltpu.make_async_copy(wxp_hbm.at[gy], wxp, lsem.at[0]),
-        pltpu.make_async_copy(cot_hbm, cot, lsem.at[1]),
-        pltpu.make_async_copy(tyi_hbm, tyi, lsem.at[2]),
-        pltpu.make_async_copy(wxi_hbm.at[gy], wxi, lsem.at[3]),
-    ]
+    pieces = [(f_hbm.at[pl.ds(r0, n)], f_ref.at[pl.ds(r0, n)]) for r0 in starts]
+    pieces.insert(0, (tyf_hbm, tyf_ref))
+    pieces += [(w_hbm, w_ref), (selw_hbm, selw_ref), (mix_hbm, mix_ref), (wxp_hbm.at[gy], wxp)]
+    pieces += [(pab_hbm, pab_ref), (px_hbm, px_ref), (wxi_hbm.at[gy], wxi), (cot_hbm, cot), (tyi_hbm, tyi)]
+    loads = [pltpu.make_async_copy(src, dst, lsem.at[k]) for k, (src, dst) in enumerate(pieces)]
     for copy in loads:
         copy.start()
+    late = dict(zip(("w", "selw", "mix", "wxp", "pab", "px", "wxi", "cot", "tyi"), loads[1 + len(starts) :]))
 
     pending = []
 
@@ -212,11 +208,6 @@
     def ex_y(src_of, dst, ex):
         return exchange("gy", GY, gy, src_of, dst, by_s, by_r, ex)
 
-    hrows = rows // 2
-    chunk = 160 if hrows % 160 == 0 else hrows
-    chunks = [[h * hrows + r for r in range(0, hrows, chunk)] for h in range(2)]
-    starts = chunks[0] + chunks[1]
-    n = chunk
     rest = jnp.zeros((8, 128), F32)
 
     def part_of(h, kk, r0):
@@ -233,8 +224,14 @@
             block = a3[pl.ds(h * 3 * hrows + g, 120, stride=G), :]
             dst[h, g] = jnp.concatenate([block, rest], axis=0).T[:32]
 
+    def to_planes(value):
+        for i in range(4):
+            gi[i] = value[:, i * 128 : (i + 1) * 128]
+
+    loads[0].wait()
     for h in range(2):
         for r0 in chunks[h]:
+            loads[1 + starts.index(r0)].wait()
             y_forward(f_ref[r0 : r0 + n, :], h, r0)
         to_groups(h, sx1)
     pl.semaphore_wait(barrier, G - 1 + GY - 1 + D - 1)
@@ -242,6 +239,8 @@
     for h in range(2):
         rx1[h, gx] = sx1[h, gx]
 
+    late["w"].wait()
+    late["selw"].wait()
     wst[...] = jnp.zeros_like(wst)
     for m in range(9):
         wst[m * 48 : m * 48 + 2 * C, 0:C] = w_ref[m].astype(F32).reshape(2 * C, C)
@@ -253,6 +252,7 @@
         wparts.append(jnp.where(cond, wexp[m * 48 : m * 48 + 48], 0.0))
     wmasked = jnp.concatenate(wparts, axis=0).astype(BF16)
     ws[...] = mm(selw_ref[...], wmasked).astype(BF16)
+    late["mix"].wait()
     mixpad[...] = jnp.zeros_like(mixpad)
     mixpad[0:C, 0:C] = mix_ref[...].astype(F32)
     mixb = mixpad[...].astype(BF16)
@@ -270,17 +270,23 @@
         bc[q] = onehot(iota((128, 512), 0) == ((lanes >> 7) + 4 * q) * 4 + (lanes & 3))
     lanes = iota((128, 512), 1)
     ohr = onehot(iota((128, 512), 0) == (lanes >> 7) * 32 + ((lanes & 127) >> 2))
+    col = iota((256, 512), 1)
+    ohg[0] = onehot(lane_code((256, 512), 24) == (col & 127) * 4 + (col >> 7))
+    ohg[1] = onehot(lane_code((256, 512), 20) == (col & 63) * 4 + (col >> 7))
 
     def x_forward(recv, send, h):
         hi, lo = hilo(recv[h].reshape(32 * G, 128))
         p = mm(wxp[0], hi) + (mm(wxp[0], lo) + mm(wxp[1], hi))
-        send[h] = p.reshape(GY, 6 * G, 128)
+        send[h] = p.astype(send.dtype).reshape(GY, 6 * G, 128)
 
     def y_sum(recv):
-        halves = [(recv[h, 0] + recv[h, 1]) + (recv[h, 2] + recv[h, 3]) for h in range(2)]
+        halves = []
+        for h in range(2):
+            p = [recv[h, k].astype(F32) for k in range(GY)]
+            halves.append((p[0] + p[1]) + (p[2] + p[3]))
         return jnp.concatenate(halves, axis=1)
 
-    loads[0].wait()
+    late["wxp"].wait()
     wait_y1 = []
     for h in range(2):
         wait_x1[h]()
@@ -291,31 +297,33 @@
     rw[gx] = ws[...]
 
     wait_w()
+    late["pab"].wait()
     rab = mm(pab_ref[...], rw[...].reshape(32 * G, 640)).astype(BF16)
     for q in range(5):
         rq[q] = mm(rab[:, q * 128 : (q + 1) * 128], ohr)
+    late["px"].wait()
 
     for h in range(2):
         wait_y1[h]()
     shi, slo = hilo(y_sum(ry1))
-    both = mm(px_ref[...], shi) + mm(px_ref[...], slo)
-    sspec[...] = both[: 8 * G].reshape(G, 8, 256)
-
-    low = iota((16 * G, 128), 1) < 40
+    spec = mm(px_ref[...], shi) + mm(px_ref[...], slo)
+    sspec[...] = spec.reshape(G, 8, 256)
+
+    low = iota((8 * G, 128), 1) < 40
     turn = lambda a, by: pltpu.roll(a, by % 128, 1) if by % 128 else a
     parts = []
     for kk in range(3):
-        h0, h1 = turn(both[:, :128], -40 * kk), turn(both[:, 128:], 40 - 40 * kk)
+        h0, h1 = turn(spec[:, :128], -40 * kk), turn(spec[:, 128:], 40 - 40 * kk)
         parts.append(jnp.where(low, h0, h1))
-    stacked = jnp.concatenate(parts, axis=0)
-    xhi, xlo = hilo(stacked)
-    acc = jnp.zeros((48 * G, 128), F32)
+    xhi, xlo = hilo(jnp.concatenate(parts, axis=0))
+    acc = [jnp.zeros((24 * G, 128), F32) for _ in range(2)]
     for q in range(5):
-        spread = (mm(xhi, bc[q]) + mm(xlo, bc[q])) * rq[q]
-        acc += (spread[:, :128] + spread[:, 128:256]) + (spread[:, 256:384] + spread[:, 384:])
-    acc = acc.reshape(3, 2, 8 * G, 128)
-    acc = acc[:, 0] + acc[:, 1]
-    low = low[: 8 * G]
+        spread = mm(xhi, bc[q]) + mm(xlo, bc[q])
+        for ab in range(2):
+            prod = spread * rq[q, ab * 24 * G : (ab + 1) * 24 * G]
+            acc[ab] += (prod[:, :128] + prod[:, 128:256]) + (prod[:, 256:384] + prod[:, 384:])
+    swapped = pltpu.roll(acc[1].reshape(3 * G, 8, 128), 4, 1).reshape(24 * G, 128)
+    acc = (acc[0] + swapped).reshape(3, 8 * G, 128)
     wait_y2 = []
     for h in range(2):
         mine = [jnp.where(low if h == 0 else ~low, acc[kk], 0.0) for kk in range(3)]
@@ -327,7 +335,7 @@
     wait_spec = ex_x(lambda peer: sspec.at[peer], rspec, 3)
     rspec[gx] = sspec[gx]
 
-    loads[3].wait()
+    late["wxi"].wait()
     wait_x2 = []
     for h in range(2):
         wait_y2[h]()
@@ -338,14 +346,18 @@
         rx2[h, gx] = sx2[h, gx]
 
     wait_spec()
+    hi, lo = hilo(rspec[...].reshape(8 * G, 256))
+    to_planes(mm(hi, ohg[0]) + mm(lo, ohg[0]))
     for tri in range(3):
-        s0 = rspec[:, tri : tri + 1, :].reshape(G, 256)
-        s1 = rspec[:, 4 + tri : 5 + tri, :].reshape(G, 256)
-        block = jnp.concatenate([s0, s1, jnp.zeros((128 - 2 * G, 256), F32)], axis=0)
-        stt[tri] = block.T
-
-    loads[1].wait()
-    loads[2].wait()
+        block = []
+        for i in range(4):
+            for ri in range(2):
+                block.append(gi[i, pl.ds(ri * 4 + tri, G, stride=8), :])
+        block.append(jnp.zeros((128 - 8 * G, 128), F32))
+        stt[tri] = jnp.concatenate(block, axis=0).T[:72]
+
+    late["cot"].wait()
+    late["tyi"].wait()
     wait_x3 = []
     for h in range(2):
         wait_x2[h]()
@@ -378,7 +390,6 @@
         hi, lo = hilo(cols)
         gmix += mm(erow_t, hi) + mm(erow_t, lo)
     mgx_s[...] = gmix
-    wait_mgx = ex_x(lambda peer: mgx_s, mgx_r, 8)
     mgx_r[gx] = gmix
 
     wait_y3 = []
@@ -388,6 +399,7 @@
         wait_y3.append(ex_y(lambda peer: sy3.at[h, peer], ry3.at[h], 4 + h))
         ry3[h, gy] = sy3[h, gy]
 
+    wait_mgx = ex_x(lambda peer: mgx_s, mgx_r, 8)
     wait_mgx()
     total = mgx_r[0]
     for k in range(1, G):
@@ -399,8 +411,7 @@
     for h in range(2):
         wait_y3[h]()
     ghi, glo = hilo(y_sum(ry3))
-    half = px_ref[0 : 8 * G, :]
-    sgs[...] = (mm(half, ghi) + mm(half, glo)).reshape(G, 8, 256)
+    sgs[...] = (mm(px_ref[...], ghi) + mm(px_ref[...], glo)).reshape(G, 8, 256)
     wait_gs = ex_x(lambda peer: sgs.at[peer], rgs, 9)
     rgs[gx] = sgs[gx]
 
@@ -412,22 +423,25 @@
     norm_out = 1.0 / math.sqrt(36 * G)
     spec_scale = norm_out / norm_in / math.sqrt(D * planes)
     wait_gs()
-    gm = key(iota((256, 512), 0)) == key(iota((256, 512), 1) & 255)
+    hi, lo = hilo(rgs[...].reshape(8 * G, 256))
+    to_planes(mm(hi, ohg[1]) + mm(lo, ohg[1]))
+    lane = iota((G, 128), 1)
+    lane24 = iota((24, 128), 1) & 63
     for tri in range(3):
-        g0 = rgs[:, tri : tri + 1, :].reshape(G, 256)
-        g1 = rgs[:, 4 + tri : 5 + tri, :].reshape(G, 256)
-        top = jnp.concatenate([g0, g1], axis=1)
-        bot = jnp.concatenate([g1, -g0], axis=1)
-        gg = jnp.concatenate([top, bot, jnp.zeros((128 - 2 * G, 512), F32)], axis=0)
+        block = []
+        for i in range(4):
+            g0 = gi[i, pl.ds(tri, G, stride=8), :]
+            g1 = gi[i, pl.ds(4 + tri, G, stride=8), :]
+            block += [jnp.where(lane < 64, g0, g1), jnp.where(lane < 64, g1, -g0)]
+        block.append(jnp.zeros((128 - 8 * G, 128), F32))
         ahi, alo = hilo(stt[tri])
-        bhi, blo = hilo(gg)
-        outer = (mm(ahi, bhi) + (mm(ahi, blo) + mm(alo, bhi)))
-        outer = jnp.where(gm, outer, 0.0)
-        ohi, olo = hilo(outer)
-        fold = mm(e1_ref[...], ohi) + mm(e1_ref[...], olo)
-        fhi, flo = hilo(fold)
-        grad = (mm(fhi, e2_ref[...]) + mm(flo, e2_ref[...])) * spec_scale
-        part[3 * tri : 3 * tri + 3] = grad.reshape(3, 8, 128)
+        bhi, blo = hilo(jnp.concatenate(block, axis=0))
+        outer = mm(ahi, bhi) + (mm(ahi, blo) + mm(alo, bhi))
+        grad = jnp.zeros((24, 128), F32)
+        for kk in range(3):
+            mine = (lane24 >= 20 * kk) & (lane24 < 20 * kk + 20)
+            grad += jnp.where(mine, outer[24 * kk : 24 * kk + 24], 0.0)
+        part[3 * tri : 3 * tri + 3] = (grad * spec_scale).reshape(3, 8, 128)
 
     def rs_copy(k, to):
         return pltpu.make_async_remote_copy(
@@ -482,7 +496,7 @@
         block = final[3 * tri : 3 * tri + 3].reshape(24, 128)
         for kk in range(3):
             for ri in range(2):
-                off = ri * 60 + kk * 20
+                off = ri * 64 + kk * 20
                 sg_ref[tri * 3 + kk, :, ri, :] = block[:C, off : off + C]
 
     for copy in pending:
@@ -498,6 +512,15 @@
     def _():
         for k in range(1, D):
             ag_copy(k, lax.rem(dp + k, D), dp).wait_send()
+
+
+def store_kernel(out, sg, mg, out_hbm, sg_hbm, mg_hbm, sems):
+    pairs = ((out, out_hbm), (sg, sg_hbm), (mg, mg_hbm))
+    copies = [pltpu.make_async_copy(src, dst, sems.at[k]) for k, (src, dst) in enumerate(pairs)]
+    for copy in copies:
+        copy.start()
+    for copy in copies:
+        copy.wait()
 
 
 def local(G, D, fields, cotangent, mix_weight, spectral_weight):
@@ -511,9 +534,16 @@
     V = pltpu.VMEM
     scratch = [
         V((rows, cells), BF16),
+        V((2, cells, 128), BF16),
+        V((9, C, 2, C), BF16),
+        V((C, C), BF16),
+        V((32, 432), BF16),
+        V((2, GY * 6 * G, 32 * G), BF16),
+        V((48 * G, 32 * G), BF16),
+        V((8 * G, 6 * G), BF16),
+        V((2, 32 * G, GY * 8 * G), BF16),
+        V((rows, cells), BF16),
         V((2, 128, cells), BF16),
-        V((2, GY * 6 * G, 32 * G), BF16),
-        V((2, 32 * G, GY * 8 * G), BF16),
         V((3 * rows, 128), F32),
         V((rows, cells), F32),
         V((128, 128), F32),
@@ -524,8 +554,8 @@
         V((2, G, 32, 128), F32),
         V((2, GY, 6 * G, 128), F32),
         V((2, GY, 6 * G, 128), F32),
-        V((2, GY, 6 * G, 128), F32),
-        V((2, GY, 6 * G, 128), F32),
+        V((2, GY, 6 * G, 128), BF16),
+        V((2, GY, 6 * G, 128), BF16),
         V((2, 8 * G, 128), BF16),
         V((2, GY, 8 * G, 128), BF16),
         V((2, G, 32, 128), BF16),
@@ -535,11 +565,13 @@
         V((432, 128), F32),
         V((5, 48 * G, 512), F32),
         V((5, 128, 512), BF16),
+        V((2, 256, 512), BF16),
+        V((4, 8 * G, 128), F32),
         V((G, 8, 256), F32),
         V((G, 8, 256), F32),
         V((G, 8, 256), F32),
         V((G, 8, 256), F32),
-        V((3, 256, 128), F32),
+        V((3, 72, 128), F32),
         V((24, 128), F32),
         V((G, 24, 128), F32),
         V((24, 128), F32),
@@ -548,7 +580,7 @@
         V((D, tpr, 8, 128), F32),
         V((nred, tpr, 8, 128), F32),
         V((tpr, 8, 128), F32),
-        pltpu.SemaphoreType.DMA((4,)),
+        pltpu.SemaphoreType.DMA((18,)),
         pltpu.SemaphoreType.DMA((10, G)),
         pltpu.SemaphoreType.DMA((10, G)),
         pltpu.SemaphoreType.DMA((7, GY)),
@@ -563,7 +595,7 @@
             V((9, C, 2, C), F32),
             V((C, C), F32),
         ),
-        in_specs=[vm] * 9 + [hbm] * 4,
+        in_specs=[hbm] * 11,
         out_specs=(vm, vm, vm),
         scratch_shapes=scratch,
         compiler_params=pltpu.CompilerParams(
@@ -571,19 +603,25 @@
         ),
     )(
         fields.reshape(rows, cells),
+        t["tyf"],
+        spectral_weight.transpose(0, 2, 1, 3),
         mix_weight,
-        spectral_weight.transpose(0, 2, 1, 3),
-        t["tyf"],
+        t["selw"],
+        t["wxp"],
+        t["pab"],
         t["px"],
-        t["pab"],
-        t["selw"],
-        t["e1"],
-        t["e2"],
+        t["wxi"],
         cotangent.reshape(rows, cells),
         t["tyi"],
-        t["wxp"],
-        t["wxi"],
     )
+    out, sg, mg = pl.pallas_call(
+        store_kernel,
+        out_shape=tuple(jax.ShapeDtypeStruct(a.shape, a.dtype) for a in (out, sg, mg)),
+        in_specs=[hbm] * 3,
+        out_specs=(hbm,) * 3,
+        scratch_shapes=[pltpu.SemaphoreType.DMA((3,))],
+        compiler_params=pltpu.CompilerParams(vmem_limit_bytes=1 << 20),
+    )(out, sg, mg)
     return out.reshape(fields.shape), sg.transpose(0, 2, 1, 3), mg
 
 

time: 74 us -> 68.2 us (0.922)
  Pallas kernels: 71.1 us -> 67.4 us
  local copies, waits for them, and re-layouts: 2.11 us -> 0 us
    pallas_call x1, Pallas kernels: 71.1 us -> 66.5 us  [local(): pl.pallas_call(functools.partial(kernel, G, D), out_shape=(V((rows, cells...]
    unnamed x3 -> x0, local copies, waits for them, and re-layouts: 2.11 us -> none
    pallas_call x0 -> x1, Pallas kernels: none -> 0.92 us  [local(): pl.pallas_call(store_kernel, out_shape=tuple((jax.ShapeDtypeStruct(a.shap...]
where the time goes in v3:
time: 68.2 us; the launch traced here: 68.1 us
  Pallas kernels  67.4 us (99%)
    pallas_call x1, Pallas kernels, local(): pl.pallas_call(functools.partial(kernel, G, D), out_shape=(V((rows, cells...  66.5 us

profile of v3, /device:TPU:1, one launch (start us, length us, event | category | flops | bytes accessed | tf_op | source)
XLA Modules:
  0.0 68.1 jit_solution(13839491815040568849)
XLA Ops:
  0.6 66.5 %shard_map.130 = (bf16[640,512]{1,0:T(8,128)(2,1)S(1)}, f32[9,20,2,20]{3,2,1,0:T(2,128)S(1)}, f32[20,20]{1,0:T(8,128)S(1)}) custom-call(bf16[640,512]{1,0:T(8,128)(2,1)} %bitcast.5, bf16[2,512,128]{2,1,0:T(8,128)(2,1)} %constant.14.clone.tyf_hbm, bf16[9,20,2,20]{3,2,1,0:T(2,128)(2,1)} %bitcast.7, bf16[20,20]{1,0:T(8,128)(2,1)} %mix_hbm.1, ...), custom_call_target="tpu_custom_call" | custom-call | tf_op jit(solution)/shard_map/pallas_call | solution.py:591
  67.2 0.9 %shard_map.131 = (bf16[640,512]{1,0:T(8,128)(2,1)}, f32[9,20,2,20]{3,2,1,0:T(2,128)}, f32[20,20]{1,0:T(8,128)}) custom-call(bf16[640,512]{1,0:T(8,128)(2,1)S(1)} %get-tuple-element.9.out, f32[9,20,2,20]{3,2,1,0:T(2,128)S(1)} %get-tuple-element.10.sg, f32[20,20]{1,0:T(8,128)S(1)} %get-tuple-element.11.mg), custom_call_target="tpu_custom_call" | custom-call | tf_op jit(solution)/shard_map/pallas_call | solution.py:617

commit v4 on v3

--- a/solution.py
+++ b/solution.py
@@ -85,8 +85,8 @@
                 selw[kk * 8 + ri * 4 + tri, q : q + 2 * C : 2] = 1
     b = lambda a: np.asarray(a, np.float32).astype(BF16)
     return dict(
-        tyf=split(tyf),
-        tyi=split(tyi),
+        tyf=np.concatenate(split(tyf)),
+        tyi=np.concatenate(split(tyi)),
         wxp=np.stack([split(w) for w in wxp]),
         wxi=np.stack([split(w) for w in wxi]),
         px=b(px),
@@ -132,9 +132,9 @@
 def gelu_parts(h):
     k = math.sqrt(2.0 / math.pi)
     hh = h * h
-    t = jnp.tanh(k * (h + 0.044715 * (hh * h)))
-    value = 0.5 * h * (1.0 + t)
-    slope = 0.5 * (1.0 + t) + 0.5 * h * (1.0 - t * t) * (k * (1.0 + 3.0 * 0.044715 * hh))
+    u = 0.5 * jnp.tanh(h * (k + (0.044715 * k) * hh)) + 0.5
+    value = h * u
+    slope = u + (value * (1.0 - u)) * (2.0 * k + (6.0 * 0.044715 * k) * hh)
     return value, slope
 
 
@@ -145,7 +145,7 @@
     sx1, rx1, sx3, rx3, sy1, ry1, sy3, ry3, sy2, ry2, sx2, rx2,
     ws, rw, wst, rq, bc, ohg, gi, sspec, rspec, sgs, rgs, stt,
     mgx_s, mgx_r, mgy_s, mgy_r, part, rsbuf, agbuf, agsrc,
-    lsem, bx_s, bx_r, by_s, by_r, dp_s, dp_r,
+    ready, go, lsem, bx_s, bx_r, by_s, by_r, dp_s, dp_r,
 ):
     rows = C * 4 * G
     planes = 4 * G
@@ -165,8 +165,12 @@
         pl.semaphore_signal(barrier, inc=1, device_id={"gx": lax.rem(gx + k, G)}, device_id_type=MESH)
     for k in range(1, GY):
         pl.semaphore_signal(barrier, inc=1, device_id={"gy": lax.rem(gy + k, GY)}, device_id_type=MESH)
-    for k in range(1, D):
-        pl.semaphore_signal(barrier, inc=1, device_id={"dp": lax.rem(dp + k, D)}, device_id_type=MESH)
+
+    @pl.when(dp == 0)
+    def _():
+        for k in range(1, D):
+            pl.semaphore_signal(barrier, inc=1, device_id={"dp": k}, device_id_type=MESH)
+
 
     pieces = [(f_hbm.at[pl.ds(r0, n)], f_ref.at[pl.ds(r0, n)]) for r0 in starts]
     pieces.insert(0, (tyf_hbm, tyf_ref))
@@ -214,7 +218,7 @@
         return pl.ds((h * 3 + kk) * hrows + r0 - h * hrows, n)
 
     def y_forward(data, h, r0):
-        a = mm(data, tyf_ref[0]) + mm(data, tyf_ref[1])
+        a = mm(jnp.concatenate([data, data], axis=1), tyf_ref[...])
         a3[part_of(h, 0, r0), :] = a
         a3[part_of(h, 1, r0), :] = pltpu.roll(a, 96, 1)
         a3[part_of(h, 2, r0), :] = pltpu.roll(a, 64, 1)
@@ -229,14 +233,25 @@
             gi[i] = value[:, i * 128 : (i + 1) * 128]
 
     loads[0].wait()
+    wait_x1 = []
     for h in range(2):
         for r0 in chunks[h]:
             loads[1 + starts.index(r0)].wait()
             y_forward(f_ref[r0 : r0 + n, :], h, r0)
         to_groups(h, sx1)
-    pl.semaphore_wait(barrier, G - 1 + GY - 1 + D - 1)
-    wait_x1 = [ex_x(lambda peer: sx1.at[h, peer], rx1.at[h], h) for h in range(2)]
-    for h in range(2):
+        if h == 0:
+
+
+            @pl.when(dp == 0)
+            def _():
+                pl.semaphore_wait(barrier, G - 1 + GY - 1)
+
+            @pl.when(dp != 0)
+            def _():
+                pl.semaphore_wait(barrier, G - 1 + GY - 1 + 1)
+                pl.semaphore_signal(ready, inc=1, device_id={"dp": 0}, device_id_type=MESH)
+
+        wait_x1.append(ex_x(lambda peer: sx1.at[h, peer], rx1.at[h], h))
         rx1[h, gx] = sx1[h, gx]
 
     late["w"].wait()
@@ -244,12 +259,13 @@
     wst[...] = jnp.zeros_like(wst)
     for m in range(9):
         wst[m * 48 : m * 48 + 2 * C, 0:C] = w_ref[m].astype(F32).reshape(2 * C, C)
-    ohd = onehot(iota((128, 640), 0) == (iota((128, 640), 1) & 31))
+    r = iota((128, 512), 1) & 127
+    fifth = lambda r: sum(jnp.where(r >= 20 * k, 1, 0) for k in range(1, 5))
+    ohd = onehot((iota((128, 512), 0) == r - 20 * fifth(r)) & (r < 100))
     wexp = mm(wst[...].astype(BF16), ohd)
-    wparts = []
-    for m in range(9):
-        cond = (iota((48, 640), 0) >> 1) == (iota((48, 640), 1) >> 5)
-        wparts.append(jnp.where(cond, wexp[m * 48 : m * 48 + 48], 0.0))
+    lane = iota((48, 512), 1)
+    cond = (iota((48, 512), 0) >> 1) == (lane >> 7) * 5 + fifth(lane & 127)
+    wparts = [jnp.where(cond, wexp[m * 48 : m * 48 + 48], 0.0) for m in range(9)]
     wmasked = jnp.concatenate(wparts, axis=0).astype(BF16)
     ws[...] = mm(selw_ref[...], wmasked).astype(BF16)
     late["mix"].wait()
@@ -265,11 +281,11 @@
         kron = jnp.where(diag, kron, 0.0).astype(BF16)
         mixed[r0 : r0 + n, :] = mm(kron, f_ref[...])
 
-    for q in range(5):
-        lanes = iota((128, 512), 1)
-        bc[q] = onehot(iota((128, 512), 0) == ((lanes >> 7) + 4 * q) * 4 + (lanes & 3))
-    lanes = iota((128, 512), 1)
-    ohr = onehot(iota((128, 512), 0) == (lanes >> 7) * 32 + ((lanes & 127) >> 2))
+    lanes = iota((128, 640), 1)
+    for q in range(4):
+        bc[q] = onehot(iota((128, 640), 0) == ((lanes >> 7) + 5 * q) * 4 + (lanes & 3))
+    row = (lanes >> 7) * 20 + ((lanes & 127) >> 2)
+    ohr = onehot((iota((128, 640), 0) == row) & ((lanes & 127) < 80))
     col = iota((256, 512), 1)
     ohg[0] = onehot(lane_code((256, 512), 24) == (col & 127) * 4 + (col >> 7))
     ohg[1] = onehot(lane_code((256, 512), 20) == (col & 63) * 4 + (col >> 7))
@@ -293,13 +309,14 @@
         x_forward(rx1, sy1, h)
         wait_y1.append(ex_y(lambda peer: sy1.at[h, peer], ry1.at[h], h))
         ry1[h, gy] = sy1[h, gy]
-    wait_w = ex_x(lambda peer: ws, rw, 2)
-    rw[gx] = ws[...]
+        if h == 0:
+            wait_w = ex_x(lambda peer: ws, rw, 2)
+            rw[gx] = ws[...]
 
     wait_w()
     late["pab"].wait()
-    rab = mm(pab_ref[...], rw[...].reshape(32 * G, 640)).astype(BF16)
-    for q in range(5):
+    rab = mm(pab_ref[...], rw[...].reshape(32 * G, 512)).astype(BF16)
+    for q in range(4):
         rq[q] = mm(rab[:, q * 128 : (q + 1) * 128], ohr)
     late["px"].wait()
 
@@ -317,11 +334,11 @@
         parts.append(jnp.where(low, h0, h1))
     xhi, xlo = hilo(jnp.concatenate(parts, axis=0))
     acc = [jnp.zeros((24 * G, 128), F32) for _ in range(2)]
-    for q in range(5):
+    for q in range(4):
         spread = mm(xhi, bc[q]) + mm(xlo, bc[q])
         for ab in range(2):
             prod = spread * rq[q, ab * 24 * G : (ab + 1) * 24 * G]
-            acc[ab] += (prod[:, :128] + prod[:, 128:256]) + (prod[:, 256:384] + prod[:, 384:])
+            acc[ab] += sum(prod[:, k * 128 : k * 128 + 128] for k in range(5))
     swapped = pltpu.roll(acc[1].reshape(3 * G, 8, 128), 4, 1).reshape(24 * G, 128)
     acc = (acc[0] + swapped).reshape(3, 8 * G, 128)
     wait_y2 = []
@@ -331,6 +348,12 @@
         sy2[h] = vals.astype(BF16)
         wait_y2.append(ex_y(lambda peer: sy2.at[h], ry2.at[h], 2 + h))
         ry2[h, gy] = sy2[h]
+
+    @pl.when(dp == 0)
+    def _():
+        pl.semaphore_wait(ready, D - 1)
+        for k in range(1, D):
+            pl.semaphore_signal(go, inc=1, device_id={"dp": k}, device_id_type=MESH)
 
     wait_spec = ex_x(lambda peer: sspec.at[peer], rspec, 3)
     rspec[gx] = sspec[gx]
@@ -369,7 +392,7 @@
             bb += pltpu.roll(a3[part_of(h, 1, r0), :], 32, 1)
             bb += pltpu.roll(a3[part_of(h, 2, r0), :], 64, 1)
             bb = bb.astype(BF16)
-            pre = (mm(bb, tyi[0]) + mm(bb, tyi[1])) + mixed[r0 : r0 + n, :]
+            pre = mm(jnp.concatenate([bb, bb], axis=1), tyi[...]) + mixed[r0 : r0 + n, :]
             value, slope = gelu_parts(pre)
             out_ref[r0 : r0 + n, :] = value.astype(BF16)
             back = (cot[r0 : r0 + n, :].astype(F32) * slope).astype(BF16)
@@ -463,6 +486,10 @@
             device_id_type=MESH,
         )
 
+    @pl.when(dp != 0)
+    def _():
+        pl.semaphore_wait(go, 1)
+
     for k in range(1, D):
         to = lax.rem(dp + k, D)
 
@@ -534,7 +561,7 @@
     V = pltpu.VMEM
     scratch = [
         V((rows, cells), BF16),
-        V((2, cells, 128), BF16),
+        V((2 * cells, 128), BF16),
         V((9, C, 2, C), BF16),
         V((C, C), BF16),
         V((32, 432), BF16),
@@ -543,7 +570,7 @@
         V((8 * G, 6 * G), BF16),
         V((2, 32 * G, GY * 8 * G), BF16),
         V((rows, cells), BF16),
-        V((2, 128, cells), BF16),
+        V((256, cells), BF16),
         V((3 * rows, 128), F32),
         V((rows, cells), F32),
         V((128, 128), F32),
@@ -560,11 +587,11 @@
         V((2, GY, 8 * G, 128), BF16),
         V((2, G, 32, 128), BF16),
         V((2, G, 32, 128), BF16),
-        V((32, 640), BF16),
-        V((G, 32, 640), BF16),
+        V((32, 512), BF16),
+        V((G, 32, 512), BF16),
         V((432, 128), F32),
-        V((5, 48 * G, 512), F32),
-        V((5, 128, 512), BF16),
+        V((4, 48 * G, 640), F32),
+        V((4, 128, 640), BF16),
         V((2, 256, 512), BF16),
         V((4, 8 * G, 128), F32),
         V((G, 8, 256), F32),
@@ -580,6 +607,8 @@
         V((D, tpr, 8, 128), F32),
         V((nred, tpr, 8, 128), F32),
         V((tpr, 8, 128), F32),
+        pltpu.SemaphoreType.REGULAR,
+        pltpu.SemaphoreType.REGULAR,
         pltpu.SemaphoreType.DMA((18,)),
         pltpu.SemaphoreType.DMA((10, G)),
         pltpu.SemaphoreType.DMA((10, G)),

time: 68.2 us -> 66.8 us (0.979)
  Pallas kernels: 67.4 us -> 66 us
    pallas_call x1, Pallas kernels: 66.5 us -> 65.1 us  [local(): pl.pallas_call(functools.partial(kernel, G, D), out_shape=(V((rows, cells...]
where the time goes in v4:
time: 66.8 us; the launch traced here: 66.7 us
  Pallas kernels  66 us (99%)
    pallas_call x1, Pallas kernels, local(): pl.pallas_call(functools.partial(kernel, G, D), out_shape=(V((rows, cells...  65.1 us

profile of v4, /device:TPU:1, one launch (start us, length us, event | category | flops | bytes accessed | tf_op | source)
XLA Modules:
  0.0 66.7 jit_solution(7097476452036782562)
XLA Ops:
  0.6 65.1 %shard_map.130 = (bf16[640,512]{1,0:T(8,128)(2,1)S(1)}, f32[9,20,2,20]{3,2,1,0:T(2,128)S(1)}, f32[20,20]{1,0:T(8,128)S(1)}) custom-call(bf16[640,512]{1,0:T(8,128)(2,1)} %bitcast.5, bf16[1024,128]{1,0:T(8,128)(2,1)} %constant.14.clone.tyf_hbm, bf16[9,20,2,20]{3,2,1,0:T(2,128)(2,1)} %bitcast.7, bf16[20,20]{1,0:T(8,128)(2,1)} %mix_hbm.1, ...), custom_call_target="tpu_custom_call" | custom-call | tf_op jit(solution)/shard_map/pallas_call | solution.py:620
  65.7 0.9 %shard_map.131 = (bf16[640,512]{1,0:T(8,128)(2,1)}, f32[9,20,2,20]{3,2,1,0:T(2,128)}, f32[20,20]{1,0:T(8,128)}) custom-call(bf16[640,512]{1,0:T(8,128)(2,1)S(1)} %get-tuple-element.9.out, f32[9,20,2,20]{3,2,1,0:T(2,128)S(1)} %get-tuple-element.10.sg, f32[20,20]{1,0:T(8,128)S(1)} %get-tuple-element.11.mg), custom_call_target="tpu_custom_call" | custom-call | tf_op jit(solution)/shard_map/pallas_call | solution.py:646

commit v5 on v4

--- a/solution.py
+++ b/solution.py
@@ -141,7 +141,7 @@
 def kernel(
     G, D, f_hbm, tyf_hbm, w_hbm, mix_hbm, selw_hbm, wxp_hbm, pab_hbm, px_hbm, wxi_hbm, cot_hbm, tyi_hbm,
     out_ref, sg_ref, mg_ref,
-    f_ref, tyf_ref, w_ref, mix_ref, selw_ref, wxp, pab_ref, px_ref, wxi, cot, tyi, a3, mixed, mixpad, backb,
+    f_ref, tyf_ref, w_ref, mix_ref, selw_ref, wxp, pab_ref, px_ref, wxi, cot, tyi, a3, b3, mixed, mixpad, backb,
     sx1, rx1, sx3, rx3, sy1, ry1, sy3, ry3, sy2, ry2, sx2, rx2,
     ws, rw, wst, rq, bc, ohg, gi, sspec, rspec, sgs, rgs, stt,
     mgx_s, mgx_r, mgy_s, mgy_r, part, rsbuf, agbuf, agsrc,
@@ -195,7 +195,7 @@
                 device_id_type=MESH,
             )
 
-        copies = [one(k) for k in range(1, size)]
+        copies = [one(k) for k in sorted(range(1, size), key=lambda k: abs(2 * k - size))]
         for copy in copies:
             copy.start()
         pending.extend(copies)
@@ -281,9 +281,11 @@
         kron = jnp.where(diag, kron, 0.0).astype(BF16)
         mixed[r0 : r0 + n, :] = mm(kron, f_ref[...])
 
+    lanes = iota((256, 640), 1)
+    for q in range(4):
+        spot = ((lanes >> 7) + 5 * q) * 4 + (lanes & 3)
+        bc[q] = onehot((iota((256, 640), 0) & 127) == spot)
     lanes = iota((128, 640), 1)
-    for q in range(4):
-        bc[q] = onehot(iota((128, 640), 0) == ((lanes >> 7) + 5 * q) * 4 + (lanes & 3))
     row = (lanes >> 7) * 20 + ((lanes & 127) >> 2)
     ohr = onehot((iota((128, 640), 0) == row) & ((lanes & 127) < 80))
     col = iota((256, 512), 1)
@@ -295,12 +297,9 @@
         p = mm(wxp[0], hi) + (mm(wxp[0], lo) + mm(wxp[1], hi))
         send[h] = p.astype(send.dtype).reshape(GY, 6 * G, 128)
 
-    def y_sum(recv):
-        halves = []
-        for h in range(2):
-            p = [recv[h, k].astype(F32) for k in range(GY)]
-            halves.append((p[0] + p[1]) + (p[2] + p[3]))
-        return jnp.concatenate(halves, axis=1)
+    def y_sum(recv, h):
+        p = [recv[h, k].astype(F32) for k in range(GY)]
+        return (p[0] + p[1]) + (p[2] + p[3])
 
     late["wxp"].wait()
     wait_y1 = []
@@ -322,7 +321,7 @@
 
     for h in range(2):
         wait_y1[h]()
-    shi, slo = hilo(y_sum(ry1))
+    shi, slo = hilo(jnp.concatenate([y_sum(ry1, h) for h in range(2)], axis=1))
     spec = mm(px_ref[...], shi) + mm(px_ref[...], slo)
     sspec[...] = spec.reshape(G, 8, 256)
 
@@ -332,10 +331,10 @@
     for kk in range(3):
         h0, h1 = turn(spec[:, :128], -40 * kk), turn(spec[:, 128:], 40 - 40 * kk)
         parts.append(jnp.where(low, h0, h1))
-    xhi, xlo = hilo(jnp.concatenate(parts, axis=0))
+    xx = jnp.concatenate(hilo(jnp.concatenate(parts, axis=0)), axis=1)
     acc = [jnp.zeros((24 * G, 128), F32) for _ in range(2)]
     for q in range(4):
-        spread = mm(xhi, bc[q]) + mm(xlo, bc[q])
+        spread = mm(xx, bc[q])
         for ab in range(2):
             prod = spread * rq[q, ab * 24 * G : (ab + 1) * 24 * G]
             acc[ab] += sum(prod[:, k * 128 : k * 128 + 128] for k in range(5))
@@ -381,23 +380,29 @@
 
     late["cot"].wait()
     late["tyi"].wait()
-    wait_x3 = []
-    for h in range(2):
+    def planes_back(h):
         wait_x2[h]()
         for g in range(G):
             block = jnp.concatenate([rx2[h, g].astype(F32), jnp.zeros((96, 128), F32)], axis=0)
-            a3[pl.ds(h * 3 * hrows + g, 120, stride=G), :] = block.T[:120]
+            b3[pl.ds(h * 3 * hrows + g, 120, stride=G), :] = block.T[:120]
+
+    def pointwise(h, r0):
+        bb = b3[part_of(h, 0, r0), :]
+        bb += pltpu.roll(b3[part_of(h, 1, r0), :], 32, 1)
+        bb += pltpu.roll(b3[part_of(h, 2, r0), :], 64, 1)
+        bb = bb.astype(BF16)
+        pre = mm(jnp.concatenate([bb, bb], axis=1), tyi[...]) + mixed[r0 : r0 + n, :]
+        value, slope = gelu_parts(pre)
+        out_ref[r0 : r0 + n, :] = value.astype(BF16)
+        back = (cot[r0 : r0 + n, :].astype(F32) * slope).astype(BF16)
+        backb[r0 : r0 + n, :] = back
+        y_forward(back, h, r0)
+
+    wait_x3 = []
+    for h in range(2):
+        planes_back(h)
         for r0 in chunks[h]:
-            bb = a3[part_of(h, 0, r0), :]
-            bb += pltpu.roll(a3[part_of(h, 1, r0), :], 32, 1)
-            bb += pltpu.roll(a3[part_of(h, 2, r0), :], 64, 1)
-            bb = bb.astype(BF16)
-            pre = mm(jnp.concatenate([bb, bb], axis=1), tyi[...]) + mixed[r0 : r0 + n, :]
-            value, slope = gelu_parts(pre)
-            out_ref[r0 : r0 + n, :] = value.astype(BF16)
-            back = (cot[r0 : r0 + n, :].astype(F32) * slope).astype(BF16)
-            backb[r0 : r0 + n, :] = back
-            y_forward(back, h, r0)
+            pointwise(h, r0)
         to_groups(h, sx3)
         wait_x3.append(ex_x(lambda peer: sx3.at[h, peer], rx3.at[h], 6 + h))
         rx3[h, gx] = sx3[h, gx]
@@ -431,12 +436,13 @@
     wait_mgy = ex_y(lambda peer: mgy_s, mgy_r, 6)
     mgy_r[gy] = total
 
+    wait_gs = []
     for h in range(2):
         wait_y3[h]()
-    ghi, glo = hilo(y_sum(ry3))
-    sgs[...] = (mm(px_ref[...], ghi) + mm(px_ref[...], glo)).reshape(G, 8, 256)
-    wait_gs = ex_x(lambda peer: sgs.at[peer], rgs, 9)
-    rgs[gx] = sgs[gx]
+        ghi, glo = hilo(y_sum(ry3, h))
+        sgs[h] = (mm(px_ref[...], ghi) + mm(px_ref[...], glo)).reshape(G, 8, 128)
+        wait_gs.append(ex_x(lambda peer: sgs.at[h, peer], rgs.at[h], 9 + h))
+        rgs[h, gx] = sgs[h, gx]
 
     wait_mgy()
     mix_scale = 1.0 / math.sqrt(D * planes * 16 * G * NY)
@@ -445,8 +451,9 @@
     norm_in = 1.0 / math.sqrt(16 * G * NY)
     norm_out = 1.0 / math.sqrt(36 * G)
     spec_scale = norm_out / norm_in / math.sqrt(D * planes)
-    wait_gs()
-    hi, lo = hilo(rgs[...].reshape(8 * G, 256))
+    for h in range(2):
+        wait_gs[h]()
+    hi, lo = hilo(jnp.concatenate([rgs[h].reshape(8 * G, 128) for h in range(2)], axis=1))
     to_planes(mm(hi, ohg[1]) + mm(lo, ohg[1]))
     lane = iota((G, 128), 1)
     lane24 = iota((24, 128), 1) & 63
@@ -510,22 +517,6 @@
             ag_copy(k, lax.rem(dp + k, D), dp).start()
         agbuf[dp] = tile
 
-    for k in range(1, D):
-        frm = lax.rem(dp + D - k, D)
-
-        @pl.when(frm < nred)
-        def _():
-            ag_copy(k, dp, frm).wait_recv()
-
-    final = agbuf[...].reshape(TILES, 8, 128)
-    mg_ref[...] = final[9:12].reshape(24, 128)[:C, :C]
-    for tri in range(3):
-        block = final[3 * tri : 3 * tri + 3].reshape(24, 128)
-        for kk in range(3):
-            for ri in range(2):
-                off = ri * 64 + kk * 20
-                sg_ref[tri * 3 + kk, :, ri, :] = block[:C, off : off + C]
-
     for copy in pending:
         copy.wait_send()
     for k in range(1, D):
@@ -534,6 +525,27 @@
         @pl.when(to < nred)
         def _():
             rs_copy(k, to).wait_send()
+
+    for k in range(1, D):
+        frm = lax.rem(dp + D - k, D)
+
+        @pl.when(frm < nred)
+        def _():
+            ag_copy(k, dp, frm).wait_recv()
+
+    final = agbuf[...].reshape(TILES, 8, 128)
+    mg_ref[...] = final[9:12].reshape(24, 128)[:C, :C]
+    pairs = iota((40, 64), 0) == (iota((40, 64), 1) & 31) * 2 + (iota((40, 64), 1) >> 5)
+    pairs = onehot(pairs)
+    gap = jnp.zeros((8, 128), F32)
+    for tri in range(3):
+        block = final[3 * tri : 3 * tri + 3].reshape(24, 128)
+        both = jnp.concatenate([block, gap, pltpu.roll(block, 64, 1), gap], axis=0)
+        hi, lo = hilo(both)
+        both = mm(pairs, hi) + mm(pairs, lo)
+        for kk in range(3):
+            piece = both if kk == 0 else pltpu.roll(both, 128 - 20 * kk, 1)
+            sg_ref[tri * 3 + kk] = piece[:, :C].reshape(C, 2, C)
 
     @pl.when(dp < nred)
     def _():
@@ -572,6 +584,7 @@
         V((rows, cells), BF16),
         V((256, cells), BF16),
         V((3 * rows, 128), F32),
+        V((3 * rows, 128), F32),
         V((rows, cells), F32),
         V((128, 128), F32),
         V((rows, cells), BF16),
@@ -591,13 +604,13 @@
         V((G, 32, 512), BF16),
         V((432, 128), F32),
         V((4, 48 * G, 640), F32),
-        V((4, 128, 640), BF16),
+        V((4, 256, 640), BF16),
         V((2, 256, 512), BF16),
         V((4, 8 * G, 128), F32),
         V((G, 8, 256), F32),
         V((G, 8, 256), F32),
-        V((G, 8, 256), F32),
-        V((G, 8, 256), F32),
+        V((2, G, 8, 128), F32),
+        V((2, G, 8, 128), F32),
         V((3, 72, 128), F32),
         V((24, 128), F32),
         V((G, 24, 128), F32),
@@ -609,9 +622,9 @@
         V((tpr, 8, 128), F32),
         pltpu.SemaphoreType.REGULAR,
         pltpu.SemaphoreType.REGULAR,
-        pltpu.SemaphoreType.DMA((18,)),
-        pltpu.SemaphoreType.DMA((10, G)),
-        pltpu.SemaphoreType.DMA((10, G)),
+        pltpu.SemaphoreType.DMA((32,)),
+        pltpu.SemaphoreType.DMA((11, G)),
+        pltpu.SemaphoreType.DMA((11, G)),
         pltpu.SemaphoreType.DMA((7, GY)),
         pltpu.SemaphoreType.DMA((7, GY)),
         pltpu.SemaphoreType.DMA((2, D)),

time: 66.8 us -> 65.5 us (0.981)
  Pallas kernels: 66 us -> 64.7 us
    pallas_call x1, Pallas kernels: 65.1 us -> 63.8 us  [local(): pl.pallas_call(functools.partial(kernel, G, D), out_shape=(V((rows, cells...]
where the time goes in v5:
time: 65.5 us; the launch traced here: 65.3 us
  Pallas kernels  64.7 us (99%)
    pallas_call x1, Pallas kernels, local(): pl.pallas_call(functools.partial(kernel, G, D), out_shape=(V((rows, cells...  63.8 us

profile of v5, /device:TPU:1, one launch (start us, length us, event | category | flops | bytes accessed | tf_op | source)
XLA Modules:
  0.0 65.3 jit_solution(14033540524667853440)
XLA Ops:
  0.6 63.8 %shard_map.130 = (bf16[640,512]{1,0:T(8,128)(2,1)S(1)}, f32[9,20,2,20]{3,2,1,0:T(2,128)S(1)}, f32[20,20]{1,0:T(8,128)S(1)}) custom-call(bf16[640,512]{1,0:T(8,128)(2,1)} %bitcast.5, bf16[1024,128]{1,0:T(8,128)(2,1)} %constant.14.clone.tyf_hbm, bf16[9,20,2,20]{3,2,1,0:T(2,128)(2,1)} %bitcast.7, bf16[20,20]{1,0:T(8,128)(2,1)} %mix_hbm.1, ...), custom_call_target="tpu_custom_call" | custom-call | tf_op jit(solution)/shard_map/pallas_call | solution.py:633
  64.4 0.9 %shard_map.131 = (bf16[640,512]{1,0:T(8,128)(2,1)}, f32[9,20,2,20]{3,2,1,0:T(2,128)}, f32[20,20]{1,0:T(8,128)}) custom-call(bf16[640,512]{1,0:T(8,128)(2,1)S(1)} %get-tuple-element.9.out, f32[9,20,2,20]{3,2,1,0:T(2,128)S(1)} %get-tuple-element.10.sg, f32[20,20]{1,0:T(8,128)S(1)} %get-tuple-element.11.mg), custom_call_target="tpu_custom_call" | custom-call | tf_op jit(solution)/shard_map/pallas_call | solution.py:659

commit v6 on v5

--- a/solution.py
+++ b/solution.py
@@ -47,7 +47,7 @@
                 tyi[col, x * NY : (x + 1) * NY] = np.cos(ang)
                 tyi[col + 1, x * NY : (x + 1) * NY] = -np.sin(ang)
     wxp = np.zeros((GY, GY * 6 * G, 32 * G))
-    wxi = np.zeros((GY, 32 * G, GY * 8 * G))
+    wxi = np.zeros((GY, 32 * G, GY * 6 * G))
     for gy in range(GY):
         for go in range(GY):
             for tri in range(3):
@@ -56,7 +56,6 @@
                     j = 3 * gq + jj
                     kx = j if j < kxn // 2 else nx - kxn + j
                     rp = go * 6 * G + gq * 6 + tri * 2
-                    ci = go * 8 * G + gq * 8 + tri
                     for gx in range(G):
                         for x in range(XL):
                             ang = 2 * np.pi * (kx * (4 * (gx * GY + gy) + x) % nx) / nx
@@ -64,8 +63,8 @@
                             k = gx * 32 + ks * 8 + x * 2
                             wxp[gy, rp, k], wxp[gy, rp, k + 1] = c, s
                             wxp[gy, rp + 1, k], wxp[gy, rp + 1, k + 1] = -s, c
-                            wxi[gy, k, ci], wxi[gy, k, ci + 4] = c * norm_out, -s * norm_out
-                            wxi[gy, k + 1, ci], wxi[gy, k + 1, ci + 4] = s * norm_out, c * norm_out
+                            wxi[gy, k, rp], wxi[gy, k, rp + 1] = c * norm_out, -s * norm_out
+                            wxi[gy, k + 1, rp], wxi[gy, k + 1, rp + 1] = s * norm_out, c * norm_out
     px = np.zeros((8 * G, 6 * G))
     pab = np.zeros((2, 3, 8 * G, 32 * G))
     for gq in range(G):
@@ -90,6 +89,7 @@
         wxp=np.stack([split(w) for w in wxp]),
         wxi=np.stack([split(w) for w in wxi]),
         px=b(px),
+        pxt=b(px.T),
         pab=b(pab.reshape(48 * G, 32 * G)),
         selw=b(selw),
     )
@@ -139,9 +139,9 @@
 
 
 def kernel(
-    G, D, f_hbm, tyf_hbm, w_hbm, mix_hbm, selw_hbm, wxp_hbm, pab_hbm, px_hbm, wxi_hbm, cot_hbm, tyi_hbm,
+    G, D, f_hbm, tyf_hbm, w_hbm, mix_hbm, selw_hbm, wxp_hbm, pab_hbm, px_hbm, pxt_hbm, wxi_hbm, cot_hbm, tyi_hbm,
     out_ref, sg_ref, mg_ref,
-    f_ref, tyf_ref, w_ref, mix_ref, selw_ref, wxp, pab_ref, px_ref, wxi, cot, tyi, a3, b3, mixed, mixpad, backb,
+    f_ref, tyf_ref, w_ref, mix_ref, selw_ref, wxp, pab_ref, px_ref, pxt_ref, wxi, cot, tyi, a3, b3, mixed, mixpad, backb,
     sx1, rx1, sx3, rx3, sy1, ry1, sy3, ry3, sy2, ry2, sx2, rx2,
     ws, rw, wst, rq, bc, ohg, gi, sspec, rspec, sgs, rgs, stt,
     mgx_s, mgx_r, mgy_s, mgy_r, part, rsbuf, agbuf, agsrc,
@@ -160,6 +160,14 @@
     chunks = [[h * hrows + r for r in range(0, hrows, chunk)] for h in range(2)]
     starts = chunks[0] + chunks[1]
     n = chunk
+    pieces = [(f_hbm.at[pl.ds(r0, n)], f_ref.at[pl.ds(r0, n)]) for r0 in starts]
+    pieces.insert(0, (tyf_hbm, tyf_ref))
+    pieces += [(w_hbm, w_ref), (selw_hbm, selw_ref), (mix_hbm, mix_ref), (wxp_hbm.at[gy], wxp)]
+    pieces += [(pab_hbm, pab_ref), (px_hbm, px_ref), (pxt_hbm, pxt_ref), (wxi_hbm.at[gy], wxi), (cot_hbm, cot), (tyi_hbm, tyi)]
+    loads = [pltpu.make_async_copy(src, dst, lsem.at[k]) for k, (src, dst) in enumerate(pieces)]
+    for copy in loads[: 1 + len(starts)]:
+        copy.start()
+
     barrier = pltpu.get_barrier_semaphore()
     for k in range(1, G):
         pl.semaphore_signal(barrier, inc=1, device_id={"gx": lax.rem(gx + k, G)}, device_id_type=MESH)
@@ -172,14 +180,9 @@
             pl.semaphore_signal(barrier, inc=1, device_id={"dp": k}, device_id_type=MESH)
 
 
-    pieces = [(f_hbm.at[pl.ds(r0, n)], f_ref.at[pl.ds(r0, n)]) for r0 in starts]
-    pieces.insert(0, (tyf_hbm, tyf_ref))
-    pieces += [(w_hbm, w_ref), (selw_hbm, selw_ref), (mix_hbm, mix_ref), (wxp_hbm.at[gy], wxp)]
-    pieces += [(pab_hbm, pab_ref), (px_hbm, px_ref), (wxi_hbm.at[gy], wxi), (cot_hbm, cot), (tyi_hbm, tyi)]
-    loads = [pltpu.make_async_copy(src, dst, lsem.at[k]) for k, (src, dst) in enumerate(pieces)]
-    for copy in loads:
+    for copy in loads[1 + len(starts) :]:
         copy.start()
-    late = dict(zip(("w", "selw", "mix", "wxp", "pab", "px", "wxi", "cot", "tyi"), loads[1 + len(starts) :]))
+    late = dict(zip(("w", "selw", "mix", "wxp", "pab", "px", "pxt", "wxi", "cot", "tyi"), loads[1 + len(starts) :]))
 
     pending = []
 
@@ -318,6 +321,7 @@
     for q in range(4):
         rq[q] = mm(rab[:, q * 128 : (q + 1) * 128], ohr)
     late["px"].wait()
+    late["pxt"].wait()
 
     for h in range(2):
         wait_y1[h]()
@@ -344,7 +348,7 @@
     for h in range(2):
         mine = [jnp.where(low if h == 0 else ~low, acc[kk], 0.0) for kk in range(3)]
         vals = sum(turn(mine[kk], 40 * kk - 40 * h) for kk in range(3))
-        sy2[h] = vals.astype(BF16)
+        sy2[h] = mm(pxt_ref[...], vals.astype(BF16)).astype(BF16)
         wait_y2.append(ex_y(lambda peer: sy2.at[h], ry2.at[h], 2 + h))
         ry2[h, gy] = sy2[h]
 
@@ -361,7 +365,7 @@
     wait_x2 = []
     for h in range(2):
         wait_y2[h]()
-        v = ry2[h].reshape(32 * G, 128)
+        v = ry2[h].reshape(24 * G, 128)
         b = mm(wxi[0], v) + mm(wxi[1], v)
         sx2[h] = b.astype(BF16).reshape(G, 32, 128)
         wait_x2.append(ex_x(lambda peer: sx2.at[h, peer], rx2.at[h], 4 + h))
@@ -497,7 +501,8 @@
     def _():
         pl.semaphore_wait(go, 1)
 
-    for k in range(1, D):
+    far = sorted(range(1, D), key=lambda k: -min(k % 8, 8 - k % 8))
+    for k in far:
         to = lax.rem(dp + k, D)
 
         @pl.when(to < nred)
@@ -513,7 +518,7 @@
         for k in range(1, D):
             tile += rsbuf[k]
         agsrc[...] = tile
-        for k in range(1, D):
+        for k in far:
             ag_copy(k, lax.rem(dp + k, D), dp).start()
         agbuf[dp] = tile
 
@@ -554,7 +559,9 @@
 
 
 def store_kernel(out, sg, mg, out_hbm, sg_hbm, mg_hbm, sems):
-    pairs = ((out, out_hbm), (sg, sg_hbm), (mg, mg_hbm))
+    step = out.shape[0] // 4
+    pairs = [(sg, sg_hbm), (mg, mg_hbm)]
+    pairs += [(out.at[pl.ds(k * step, step)], out_hbm.at[pl.ds(k * step, step)]) for k in range(4)]
     copies = [pltpu.make_async_copy(src, dst, sems.at[k]) for k, (src, dst) in enumerate(pairs)]
     for copy in copies:
         copy.start()
@@ -580,7 +587,8 @@
         V((2, GY * 6 * G, 32 * G), BF16),
         V((48 * G, 32 * G), BF16),
         V((8 * G, 6 * G), BF16),
-        V((2, 32 * G, GY * 8 * G), BF16),
+        V((6 * G, 8 * G), BF16),
+        V((2, 32 * G, GY * 6 * G), BF16),
         V((rows, cells), BF16),
         V((256, cells), BF16),
         V((3 * rows, 128), F32),
@@ -596,8 +604,8 @@
         V((2, GY, 6 * G, 128), F32),
         V((2, GY, 6 * G, 128), BF16),
         V((2, GY, 6 * G, 128), BF16),
-        V((2, 8 * G, 128), BF16),
-        V((2, GY, 8 * G, 128), BF16),
+        V((2, 6 * G, 128), BF16),
+        V((2, GY, 6 * G, 128), BF16),
         V((2, G, 32, 128), BF16),
         V((2, G, 32, 128), BF16),
         V((32, 512), BF16),
@@ -637,7 +645,7 @@
             V((9, C, 2, C), F32),
             V((C, C), F32),
         ),
-        in_specs=[hbm] * 11,
+        in_specs=[hbm] * 12,
         out_specs=(vm, vm, vm),
         scratch_shapes=scratch,
         compiler_params=pltpu.CompilerParams(
@@ -652,6 +660,7 @@
         t["wxp"],
         t["pab"],
         t["px"],
+        t["pxt"],
         t["wxi"],
         cotangent.reshape(rows, cells),
         t["tyi"],
@@ -661,7 +670,7 @@
         out_shape=tuple(jax.ShapeDtypeStruct(a.shape, a.dtype) for a in (out, sg, mg)),
         in_specs=[hbm] * 3,
         out_specs=(hbm,) * 3,
-        scratch_shapes=[pltpu.SemaphoreType.DMA((3,))],
+        scratch_shapes=[pltpu.SemaphoreType.DMA((6,))],
         compiler_params=pltpu.CompilerParams(vmem_limit_bytes=1 << 20),
     )(out, sg, mg)
     return out.reshape(fields.shape), sg.transpose(0, 2, 1, 3), mg

time: 65.5 us -> 64.8 us (0.989)
  Pallas kernels: 64.7 us -> 63.7 us
    pallas_call x1, Pallas kernels: 63.8 us -> 62.8 us  [local(): pl.pallas_call(functools.partial(kernel, G, D), out_shape=(V((rows, cells...]
where the time goes in v6:
time: 64.8 us; the launch traced here: 64.4 us
  Pallas kernels  63.7 us (98%)
    pallas_call x1, Pallas kernels, local(): pl.pallas_call(functools.partial(kernel, G, D), out_shape=(V((rows, cells...  62.8 us

profile of v6, /device:TPU:1, one launch (start us, length us, event | category | flops | bytes accessed | tf_op | source)
XLA Modules:
  0.0 64.4 jit_solution(10755600946101455695)
XLA Ops:
  0.6 62.8 %shard_map.139 = (bf16[640,512]{1,0:T(8,128)(2,1)S(1)}, f32[9,20,2,20]{3,2,1,0:T(2,128)S(1)}, f32[20,20]{1,0:T(8,128)S(1)}) custom-call(bf16[640,512]{1,0:T(8,128)(2,1)} %bitcast.5, bf16[1024,128]{1,0:T(8,128)(2,1)} %constant.16.clone.tyf_hbm, bf16[9,20,2,20]{3,2,1,0:T(2,128)(2,1)} %bitcast.7, bf16[20,20]{1,0:T(8,128)(2,1)} %mix_hbm.1, ...), custom_call_target="tpu_custom_call" | custom-call | tf_op jit(solution)/shard_map/pallas_call | solution.py:641
  63.4 0.9 %shard_map.140 = (bf16[640,512]{1,0:T(8,128)(2,1)}, f32[9,20,2,20]{3,2,1,0:T(2,128)}, f32[20,20]{1,0:T(8,128)}) custom-call(bf16[640,512]{1,0:T(8,128)(2,1)S(1)} %get-tuple-element.9.out, f32[9,20,2,20]{3,2,1,0:T(2,128)S(1)} %get-tuple-element.10.sg, f32[20,20]{1,0:T(8,128)S(1)} %get-tuple-element.11.mg), custom_call_target="tpu_custom_call" | custom-call | tf_op jit(solution)/shard_map/pallas_call | solution.py:668

commit v7 on v6

--- a/solution.py
+++ b/solution.py
@@ -156,7 +156,7 @@
     nred = TILES // tpr
 
     hrows = rows // 2
-    chunk = 160 if hrows % 160 == 0 else hrows
+    chunk = hrows
     chunks = [[h * hrows + r for r in range(0, hrows, chunk)] for h in range(2)]
     starts = chunks[0] + chunks[1]
     n = chunk

time: 64.8 us -> 64.8 us (level)
  no operation moved by 1% of the time
where the time goes in v7:
time: 64.8 us; the launch traced here: 64.4 us
  Pallas kernels  63.8 us (98%)
    pallas_call x1, Pallas kernels, local(): pl.pallas_call(functools.partial(kernel, G, D), out_shape=(V((rows, cells...  62.8 us

profile of v7, /device:TPU:1, one launch (start us, length us, event | category | flops | bytes accessed | tf_op | source)
XLA Modules:
  0.0 64.4 jit_solution(1476157595880544492)
XLA Ops:
  0.6 62.8 %shard_map.139 = (bf16[640,512]{1,0:T(8,128)(2,1)S(1)}, f32[9,20,2,20]{3,2,1,0:T(2,128)S(1)}, f32[20,20]{1,0:T(8,128)S(1)}) custom-call(bf16[640,512]{1,0:T(8,128)(2,1)} %bitcast.5, bf16[1024,128]{1,0:T(8,128)(2,1)} %constant.16.clone.tyf_hbm, bf16[9,20,2,20]{3,2,1,0:T(2,128)(2,1)} %bitcast.7, bf16[20,20]{1,0:T(8,128)(2,1)} %mix_hbm.1, ...), custom_call_target="tpu_custom_call" | custom-call | tf_op jit(solution)/shard_map/pallas_call | solution.py:641
  63.5 0.9 %shard_map.140 = (bf16[640,512]{1,0:T(8,128)(2,1)}, f32[9,20,2,20]{3,2,1,0:T(2,128)}, f32[20,20]{1,0:T(8,128)}) custom-call(bf16[640,512]{1,0:T(8,128)(2,1)S(1)} %get-tuple-element.9.out, f32[9,20,2,20]{3,2,1,0:T(2,128)S(1)} %get-tuple-element.10.sg, f32[20,20]{1,0:T(8,128)S(1)} %get-tuple-element.11.mg), custom_call_target="tpu_custom_call" | custom-call | tf_op jit(solution)/shard_map/pallas_call | solution.py:668

commit v8 on v6

--- a/solution.py
+++ b/solution.py
@@ -308,12 +308,12 @@
     wait_y1 = []
     for h in range(2):
         wait_x1[h]()
+        if h == 0:
+            wait_w = ex_x(lambda peer: ws, rw, 2)
+            rw[gx] = ws[...]
         x_forward(rx1, sy1, h)
         wait_y1.append(ex_y(lambda peer: sy1.at[h, peer], ry1.at[h], h))
         ry1[h, gy] = sy1[h, gy]
-        if h == 0:
-            wait_w = ex_x(lambda peer: ws, rw, 2)
-            rw[gx] = ws[...]
 
     wait_w()
     late["pab"].wait()

time: 64.8 us -> 64.6 us (level)
  no operation moved by 1% of the time
where the time goes in v8:
time: 64.6 us; the launch traced here: 64.2 us
  Pallas kernels  63.6 us (98%)
    pallas_call x1, Pallas kernels, local(): pl.pallas_call(functools.partial(kernel, G, D), out_shape=(V((rows, cells...  62.6 us

profile of v8, /device:TPU:1, one launch (start us, length us, event | category | flops | bytes accessed | tf_op | source)
XLA Modules:
  0.0 64.2 jit_solution(16981199137519184405)
XLA Ops:
  0.6 62.6 %shard_map.139 = (bf16[640,512]{1,0:T(8,128)(2,1)S(1)}, f32[9,20,2,20]{3,2,1,0:T(2,128)S(1)}, f32[20,20]{1,0:T(8,128)S(1)}) custom-call(bf16[640,512]{1,0:T(8,128)(2,1)} %bitcast.5, bf16[1024,128]{1,0:T(8,128)(2,1)} %constant.16.clone.tyf_hbm, bf16[9,20,2,20]{3,2,1,0:T(2,128)(2,1)} %bitcast.7, bf16[20,20]{1,0:T(8,128)(2,1)} %mix_hbm.1, ...), custom_call_target="tpu_custom_call" | custom-call | tf_op jit(solution)/shard_map/pallas_call | solution.py:641
  63.3 0.9 %shard_map.140 = (bf16[640,512]{1,0:T(8,128)(2,1)}, f32[9,20,2,20]{3,2,1,0:T(2,128)}, f32[20,20]{1,0:T(8,128)}) custom-call(bf16[640,512]{1,0:T(8,128)(2,1)S(1)} %get-tuple-element.9.out, f32[9,20,2,20]{3,2,1,0:T(2,128)S(1)} %get-tuple-element.10.sg, f32[20,20]{1,0:T(8,128)S(1)} %get-tuple-element.11.mg), custom_call_target="tpu_custom_call" | custom-call | tf_op jit(solution)/shard_map/pallas_call | solution.py:668
